TPU v7x, 32 devices: a whole 2x2x4 slice. The times are simulated.
32 devices in a mesh: dom: 32 (over z, y, x, core).
Axes of the slice: x: 2, y: 2, z: 4, core: 2. Of those that a mesh axis runs over, the one named last changes fastest.
Arguments:
- features: bfloat16 [65536, 256], P('dom'), may hold values from -6 to 6
- self_weight: bfloat16 [256, 256], replicated, may hold values from -0.375 to 0.375
- neighbour_weight: bfloat16 [256, 256], replicated, may hold values from -0.375 to 0.375
- send_lists: int32 [32, 32, 8], P('dom'), may hold values from 0 to 2047
- hub_nodes: int32 [32, 8], P('dom'), may hold values from 0 to 2047
- neighbours: int32 [65536, 16], P('dom'), may hold values from 0 to 2559
- counts: int32 [65536], P('dom'), may hold values from 1 to 16
- cotangent: bfloat16 [65536, 256], P('dom'), may hold values from -6 to 6
Outputs:
- activations: bfloat16 [65536, 256], P('dom')
- grad_features: float32 [65536, 256], P('dom')
- grad_weights: float32 [512, 256], P('dom')
All inputs are finite; a program needn't handle non-finite values.
Results may differ from a plain program's by a relative error of at most 0.0032.
Values may be sent and summed in bfloat16 or wider, within the bound.
A program may use at most 64 MiB of HBM per device.

v0:
```python
import jax
import jax.numpy as jnp
from jax import lax
from jax.sharding import PartitionSpec as P


def slot_counts(index, usable, width):
    columns = jnp.arange(width, dtype=jnp.int32)
    hits = (index[:, :, None] == columns[None, None, :]) & usable[:, :, None]
    return jnp.sum(hits.astype(jnp.float32), axis=1)


def gather_sum(source_rows, index, usable):
    node_rows = index.shape[0]
    block_rows = min(512, node_rows)
    blocks = node_rows // block_rows
    index_blocks = index.reshape(blocks, block_rows, index.shape[1])
    usable_blocks = usable.reshape(blocks, block_rows, usable.shape[1])
    width = source_rows.shape[0]

    def gather_one_block(block_args):
        block_index, block_usable = block_args
        weights = slot_counts(block_index, block_usable, width).astype(jnp.bfloat16)
        return jnp.dot(weights, source_rows, preferred_element_type=jnp.float32)

    summed = lax.map(gather_one_block, (index_blocks, usable_blocks))
    return summed.reshape(node_rows, source_rows.shape[1])


def scatter_rows(table_size, index, usable, edge_weight):
    node_rows = index.shape[0]
    block_rows = min(512, node_rows)
    blocks = node_rows // block_rows
    index_blocks = index.reshape(blocks, block_rows, index.shape[1])
    usable_blocks = usable.reshape(blocks, block_rows, usable.shape[1])
    weight_blocks = edge_weight.reshape(blocks, block_rows, edge_weight.shape[1])

    def scatter_one_block(running, block_args):
        block_index, block_usable, block_weight = block_args
        weights = slot_counts(block_index, block_usable, table_size)
        added = lax.dot_general(
            weights,
            block_weight,
            (((0,), (0,)), ((), ())),
            precision=lax.Precision.HIGHEST,
            preferred_element_type=jnp.float32,
        )
        return (running + added, None)

    initial = jnp.zeros((table_size, edge_weight.shape[1]), jnp.float32)
    result, unused = lax.scan(
        scatter_one_block, initial, (index_blocks, usable_blocks, weight_blocks)
    )
    return result


def body(
    features, self_weight, neighbour_weight, send_lists, hub_nodes, neighbours, counts, cotangent
):
    node_dev = features.shape[0]
    feature_width = features.shape[1]
    peer_count = lax.axis_size("dom")
    per_peer = send_lists.shape[2]
    hub_count = hub_nodes.shape[1]
    lists_flat = send_lists[0].reshape(-1)
    hub_ids = hub_nodes[0]
    outgoing = jnp.take(features, lists_flat, axis=0).reshape(peer_count, per_peer, feature_width)
    hub_local = jnp.take(features, hub_ids, axis=0)
    repeated = jnp.broadcast_to(hub_local[None], (peer_count, hub_count, feature_width))
    packed = jnp.concatenate([outgoing, repeated], axis=1)
    arrived = lax.all_to_all(packed, "dom", split_axis=0, concat_axis=0, tiled=True)
    received = arrived[:, :per_peer]
    hub_table = arrived[:, per_peer:].reshape(peer_count * hub_count, feature_width)
    remote_rows = jnp.concatenate(
        [received.reshape(peer_count * per_peer, feature_width), hub_table], axis=0
    )
    usable = jnp.arange(neighbours.shape[1], dtype=jnp.int32)[None, :] < counts[:, None]
    remote_index = neighbours - node_dev
    summed = gather_sum(features, neighbours, usable) + gather_sum(
        remote_rows, remote_index, usable
    )
    degree = counts.astype(jnp.float32)[:, None]
    mean = (summed / degree).astype(jnp.bfloat16)
    pre = jnp.dot(features, self_weight, preferred_element_type=jnp.float32) + jnp.dot(
        mean, neighbour_weight, preferred_element_type=jnp.float32
    )
    sigmoid_pre = jax.nn.sigmoid(pre)
    activations = (pre * sigmoid_pre).astype(jnp.bfloat16)
    grad_pre = (
        cotangent.astype(jnp.float32) * sigmoid_pre * (1.0 + pre * (1.0 - sigmoid_pre))
    ).astype(jnp.bfloat16)
    back_dims = (((1,), (1,)), ((), ()))
    grad_mean = lax.dot_general(
        grad_pre, neighbour_weight, back_dims, preferred_element_type=jnp.float32
    )
    grad_self = lax.dot_general(
        grad_pre, self_weight, back_dims, preferred_element_type=jnp.float32
    )
    edge_weight = grad_mean / degree
    remote_size = remote_rows.shape[0]
    local_grads = scatter_rows(node_dev, neighbours, usable, edge_weight)
    remote_grads = scatter_rows(remote_size, remote_index, usable, edge_weight)
    boundary_part = remote_grads[: peer_count * per_peer].reshape(
        peer_count, per_peer, feature_width
    )
    hub_part = remote_grads[peer_count * per_peer :]
    packed_grads = jnp.concatenate(
        [boundary_part, hub_part.reshape(peer_count, hub_count, feature_width)], axis=1
    )
    returned = lax.all_to_all(
        packed_grads.astype(jnp.bfloat16), "dom", split_axis=0, concat_axis=0, tiled=True
    ).astype(packed_grads.dtype)
    boundary_back = returned[:, :per_peer]
    hub_back = jnp.sum(returned[:, per_peer:], axis=0)
    grad_features = grad_self + local_grads
    grad_features = grad_features.at[lists_flat].add(
        boundary_back.reshape(peer_count * per_peer, feature_width)
    )
    grad_features = grad_features.at[hub_ids].add(hub_back)
    stacked = jnp.concatenate([features, mean], axis=1)
    grad_weights = lax.psum_scatter(
        lax.dot_general(
            stacked, grad_pre, (((0,), (0,)), ((), ())), preferred_element_type=jnp.float32
        ),
        "dom",
        scatter_dimension=0,
        tiled=True,
    )
    return (activations, grad_features, grad_weights)


def solution(mesh):
    in_specs = (
        P("dom", None),
        P(),
        P(),
        P("dom", None, None),
        P("dom", None),
        P("dom", None),
        P("dom"),
        P("dom", None),
    )
    out_specs = (P("dom", None), P("dom", None), P("dom", None))
    return jax.shard_map(body, mesh=mesh, in_specs=in_specs, out_specs=out_specs, check_vma=False)
```

profile of v0, /device:TPU:0, one launch (start us, length us, event | category | flops | bytes accessed | tf_op | source)
XLA Modules:
  0.0 348.4 jit_solution(97989355255736844)
XLA Ops:
  10.2 1.9 gather_fusion.1
  12.2 2.3 gather_fusion
  15.4 7.3 %all-to-all-start = ((bf16[32,16,256]{2,1,0:T(8,128)(2,1)}), bf16[32,16,256]{2,1,0:T(8,128)(2,1)S(1)}, u32[]{:S(2)}, u32[]{:S(2)}) async-start(bf16[32,16,256]{2,1,0:T(8,128)(2,1)} %pad_maximum_fusion), calls=%async_computation | async-start | bytes 524288 | tf_op jit(solution)/shard_map/all_to_all | solution.py:71
  22.9 1.5 broadcast.91.clone
  24.4 92.6 %while.42 = (s32[]{:T(128)}, f32[4,512,256]{2,1,0:T(8,128)}, s32[4,512,16]{1,2,0:T(8,128)S(1)}, pred[4,512,16]{1,2,0:T(8,128)(4,1)S(1)}, bf16[2048,256]{1,0:T(8,128)(2,1)S(1)}, /*index=5*/s32[]{:T(128)}) while((s32[]{:T(128)}, f32[4,512,256]{2,1,0:T(8,128)}, s32[4,512,16]{1,2,0:T(8,128)S(1)}, pred[4,512,16]{1,2,0:T(8,128)(4,1)S(1)}, ...), condition=%wide.region_2.3_spmd, body=%wide.region_0.0_spmd.sunk | while | flops 602931200 | bytes 5972057 | solution.py:26
  24.7 21.3 %convert_reduce_fusion.8 = bf16[512,2048]{1,0:T(8,128)(2,1)S(1)} fusion(s32[512,16]{1,0:T(8,128)S(1)} %copy.54, pred[512,16]{1,0:T(8,128)(4,1)S(1)} %copy.55), kind=kLoop, calls=%fused_computation.4.clone.1 | loop fusion | flops 66060288 | bytes 2138112 | tf_op jit(solution)/shard_map/while/body/eval_jaxpr/reduce_sum | solution.py:10
  46.0 1.5 fusion.56
  47.9 21.3 %convert_reduce_fusion.8 = bf16[512,2048]{1,0:T(8,128)(2,1)S(1)} fusion(s32[512,16]{1,0:T(8,128)S(1)} %copy.54, pred[512,16]{1,0:T(8,128)(4,1)S(1)} %copy.55), kind=kLoop, calls=%fused_computation.4.clone.1 | loop fusion | flops 66060288 | bytes 2138112 | tf_op jit(solution)/shard_map/while/body/eval_jaxpr/reduce_sum | solution.py:10
  69.2 1.5 fusion.56
  71.0 21.3 %convert_reduce_fusion.8 = bf16[512,2048]{1,0:T(8,128)(2,1)S(1)} fusion(s32[512,16]{1,0:T(8,128)S(1)} %copy.54, pred[512,16]{1,0:T(8,128)(4,1)S(1)} %copy.55), kind=kLoop, calls=%fused_computation.4.clone.1 | loop fusion | flops 66060288 | bytes 2138112 | tf_op jit(solution)/shard_map/while/body/eval_jaxpr/reduce_sum | solution.py:10
  92.3 1.6 fusion.56
  94.2 21.3 %convert_reduce_fusion.8 = bf16[512,2048]{1,0:T(8,128)(2,1)S(1)} fusion(s32[512,16]{1,0:T(8,128)S(1)} %copy.54, pred[512,16]{1,0:T(8,128)(4,1)S(1)} %copy.55), kind=kLoop, calls=%fused_computation.4.clone.1 | loop fusion | flops 66060288 | bytes 2138112 | tf_op jit(solution)/shard_map/while/body/eval_jaxpr/reduce_sum | solution.py:10
  115.5 1.5 fusion.56
  117.7 3.0 fusion.28
  120.8 1.5 broadcast.91.clone.1
  122.2 29.8 %while.43 = (s32[]{:T(128)}, f32[4,512,256]{2,1,0:T(8,128)}, s32[4,512,16]{1,2,0:T(8,128)}, pred[4,512,16]{1,2,0:T(8,128)(4,1)S(1)}, bf16[512,256]{1,0:T(8,128)(2,1)S(1)}, /*index=5*/s32[]{:T(128)}) while((s32[]{:T(128)}, f32[4,512,256]{2,1,0:T(8,128)}, s32[4,512,16]{1,2,0:T(8,128)}, pred[4,512,16]{1,2,0:T(8,128)(4,1)S(1)}, ...), condition=%wide.region_5.6_spmd, body=%wide.region_3.5_spmd.sunk | while | flops 150732800 | bytes 2039897 | solution.py:26
  123.3 5.3 %convert_reduce_fusion.9 = bf16[512,512]{1,0:T(8,128)(2,1)S(1)} fusion(s32[512,16]{1,0:T(8,128)S(1)} %copy.56, pred[512,16]{1,0:T(8,128)(4,1)S(1)} %copy.57), kind=kLoop, calls=%fused_computation.13.clone.1 | loop fusion | flops 16515072 | bytes 565248 | tf_op jit(solution)/shard_map/while/body/eval_jaxpr/reduce_sum | solution.py:10
  130.7 5.3 %convert_reduce_fusion.9 = bf16[512,512]{1,0:T(8,128)(2,1)S(1)} fusion(s32[512,16]{1,0:T(8,128)S(1)} %copy.56, pred[512,16]{1,0:T(8,128)(4,1)S(1)} %copy.57), kind=kLoop, calls=%fused_computation.13.clone.1 | loop fusion | flops 16515072 | bytes 565248 | tf_op jit(solution)/shard_map/while/body/eval_jaxpr/reduce_sum | solution.py:10
  136.0 1.1 fusion.59
  138.2 5.3 %convert_reduce_fusion.9 = bf16[512,512]{1,0:T(8,128)(2,1)S(1)} fusion(s32[512,16]{1,0:T(8,128)S(1)} %copy.56, pred[512,16]{1,0:T(8,128)(4,1)S(1)} %copy.57), kind=kLoop, calls=%fused_computation.13.clone.1 | loop fusion | flops 16515072 | bytes 565248 | tf_op jit(solution)/shard_map/while/body/eval_jaxpr/reduce_sum | solution.py:10
  145.6 5.3 %convert_reduce_fusion.9 = bf16[512,512]{1,0:T(8,128)(2,1)S(1)} fusion(s32[512,16]{1,0:T(8,128)S(1)} %copy.56, pred[512,16]{1,0:T(8,128)(4,1)S(1)} %copy.57), kind=kLoop, calls=%fused_computation.13.clone.1 | loop fusion | flops 16515072 | bytes 565248 | tf_op jit(solution)/shard_map/while/body/eval_jaxpr/reduce_sum | solution.py:10
  152.0 2.5 add.89
  154.9 1.2 copy-done.3
  156.4 2.2 multiply_convert_fusion
  159.6 1.6 fusion.20
  161.2 3.0 convolution_divide_fusion
  164.2 37.3 %while.45 = (s32[]{:T(128)}, f32[512,256]{1,0:T(8,128)S(1)}, s32[4,512,16]{1,2,0:T(8,128)}, pred[4,512,16]{1,2,0:T(8,128)(4,1)S(1)}, f32[4,512,256]{2,1,0:T(8,128)}, /*index=5*/s32[]{:T(128)}, s32[]{:T(128)}) while((s32[]{:T(128)}, f32[512,256]{1,0:T(8,128)S(1)}, s32[4,512,16]{1,2,0:T(8,128)}, ...), condition=%wide.region_11.12_spmd.clone, body=%wide.region_9.11_spmd.clone.sunk | while | flops 822083584 | bytes 3874923 | solution.py:51
  165.3 5.2 %convert_reduce_fusion.11 = f32[512,512]{1,0:T(8,128)S(1)} fusion(s32[512,16]{1,0:T(8,128)S(1)} %copy.60, pred[512,16]{1,0:T(8,128)(4,1)S(1)} %copy.61), kind=kLoop, calls=%fused_computation.30.clone.1 | loop fusion | flops 16515072 | bytes 1089536 | tf_op jit(solution)/shard_map/while/body/eval_jaxpr/reduce_sum | solution.py:10
  170.5 3.0 convolution_add_fusion.7
  174.6 5.2 %convert_reduce_fusion.11 = f32[512,512]{1,0:T(8,128)S(1)} fusion(s32[512,16]{1,0:T(8,128)S(1)} %copy.60, pred[512,16]{1,0:T(8,128)(4,1)S(1)} %copy.61), kind=kLoop, calls=%fused_computation.30.clone.1 | loop fusion | flops 16515072 | bytes 1089536 | tf_op jit(solution)/shard_map/while/body/eval_jaxpr/reduce_sum | solution.py:10
  179.9 3.0 convolution_add_fusion.7
  184.0 5.2 %convert_reduce_fusion.11 = f32[512,512]{1,0:T(8,128)S(1)} fusion(s32[512,16]{1,0:T(8,128)S(1)} %copy.60, pred[512,16]{1,0:T(8,128)(4,1)S(1)} %copy.61), kind=kLoop, calls=%fused_computation.30.clone.1 | loop fusion | flops 16515072 | bytes 1089536 | tf_op jit(solution)/shard_map/while/body/eval_jaxpr/reduce_sum | solution.py:10
  189.2 3.0 convolution_add_fusion.7
  193.3 5.2 %convert_reduce_fusion.11 = f32[512,512]{1,0:T(8,128)S(1)} fusion(s32[512,16]{1,0:T(8,128)S(1)} %copy.60, pred[512,16]{1,0:T(8,128)(4,1)S(1)} %copy.61), kind=kLoop, calls=%fused_computation.30.clone.1 | loop fusion | flops 16515072 | bytes 1089536 | tf_op jit(solution)/shard_map/while/body/eval_jaxpr/reduce_sum | solution.py:10
  198.5 3.0 convolution_add_fusion.7
  202.3 5.8 %all-to-all-start.1 = ((bf16[32,16,256]{2,1,0:T(8,128)(2,1)}), bf16[32,16,256]{2,1,0:T(8,128)(2,1)S(1)}, u32[]{:S(2)}, u32[]{:S(2)}) async-start(bf16[32,16,256]{2,1,0:T(8,128)(2,1)} %pad_maximum_fusion.2), calls=%async_computation.1 | async-start | bytes 524288 | tf_op jit(solution)/shard_map/all_to_all | solution.py:110
  208.1 122.1 %while.44 = (s32[]{:T(128)}, f32[2048,256]{1,0:T(8,128)S(1)}, s32[4,512,16]{1,2,0:T(8,128)S(1)}, pred[4,512,16]{1,2,0:T(8,128)(4,1)S(1)}, f32[4,512,256]{2,1,0:T(8,128)}, /*index=5*/s32[]{:T(128)}, s32[]{:T(128)}) while((s32[]{:T(128)}, f32[2048,256]{1,0:T(8,128)S(1)}, s32[4,512,16]{1,2,0:T(8,128)S(1)}, ...), condition=%wide.region_8.9_spmd.clone, body=%wide.region_6.8_spmd.clone.sunk | while | flops 3288334336 | bytes 13312107 | solution.py:51
  208.5 21.2 %convert_reduce_fusion.10 = f32[512,2048]{1,0:T(8,128)S(1)} fusion(s32[512,16]{1,0:T(8,128)S(1)} %copy.58, pred[512,16]{1,0:T(8,128)(4,1)S(1)} %copy.59), kind=kLoop, calls=%fused_computation.21.clone.1 | loop fusion | flops 66060288 | bytes 4235264 | tf_op jit(solution)/shard_map/while/body/eval_jaxpr/reduce_sum | solution.py:10
  229.7 9.0 %convolution_add_fusion.6 = f32[2048,256]{1,0:T(8,128)S(1)} fusion(f32[512,2048]{1,0:T(8,128)S(1)} %convert_reduce_fusion.10, f32[2048,256]{1,0:T(8,128)S(1)} %get-tuple-element.405, pred[]{:T(512)S(6)} %compare.6, f32[4,512,256]{2,1,0:T(8,128)} %get-tuple-element.415, s32[]{:T(128)S(6)} %copy.78), kind=kOutput, calls=%fused_computation.24.clone.1 | convolution fusion | flops 3222274048 | bytes 8912901 | tf_op jit(solution)/shard_map/while/body/eval_jaxpr/dot_general | solution.py:41
  239.0 21.2 %convert_reduce_fusion.10 = f32[512,2048]{1,0:T(8,128)S(1)} fusion(s32[512,16]{1,0:T(8,128)S(1)} %copy.58, pred[512,16]{1,0:T(8,128)(4,1)S(1)} %copy.59), kind=kLoop, calls=%fused_computation.21.clone.1 | loop fusion | flops 66060288 | bytes 4235264 | tf_op jit(solution)/shard_map/while/body/eval_jaxpr/reduce_sum | solution.py:10
  260.2 9.0 %convolution_add_fusion.6 = f32[2048,256]{1,0:T(8,128)S(1)} fusion(f32[512,2048]{1,0:T(8,128)S(1)} %convert_reduce_fusion.10, f32[2048,256]{1,0:T(8,128)S(1)} %get-tuple-element.405, pred[]{:T(512)S(6)} %compare.6, f32[4,512,256]{2,1,0:T(8,128)} %get-tuple-element.415, s32[]{:T(128)S(6)} %copy.78), kind=kOutput, calls=%fused_computation.24.clone.1 | convolution fusion | flops 3222274048 | bytes 8912901 | tf_op jit(solution)/shard_map/while/body/eval_jaxpr/dot_general | solution.py:41
  269.6 21.2 %convert_reduce_fusion.10 = f32[512,2048]{1,0:T(8,128)S(1)} fusion(s32[512,16]{1,0:T(8,128)S(1)} %copy.58, pred[512,16]{1,0:T(8,128)(4,1)S(1)} %copy.59), kind=kLoop, calls=%fused_computation.21.clone.1 | loop fusion | flops 66060288 | bytes 4235264 | tf_op jit(solution)/shard_map/while/body/eval_jaxpr/reduce_sum | solution.py:10
  290.7 9.0 %convolution_add_fusion.6 = f32[2048,256]{1,0:T(8,128)S(1)} fusion(f32[512,2048]{1,0:T(8,128)S(1)} %convert_reduce_fusion.10, f32[2048,256]{1,0:T(8,128)S(1)} %get-tuple-element.405, pred[]{:T(512)S(6)} %compare.6, f32[4,512,256]{2,1,0:T(8,128)} %get-tuple-element.415, s32[]{:T(128)S(6)} %copy.78), kind=kOutput, calls=%fused_computation.24.clone.1 | convolution fusion | flops 3222274048 | bytes 8912901 | tf_op jit(solution)/shard_map/while/body/eval_jaxpr/dot_general | solution.py:41
  300.1 21.2 %convert_reduce_fusion.10 = f32[512,2048]{1,0:T(8,128)S(1)} fusion(s32[512,16]{1,0:T(8,128)S(1)} %copy.58, pred[512,16]{1,0:T(8,128)(4,1)S(1)} %copy.59), kind=kLoop, calls=%fused_computation.21.clone.1 | loop fusion | flops 66060288 | bytes 4235264 | tf_op jit(solution)/shard_map/while/body/eval_jaxpr/reduce_sum | solution.py:10
  321.3 9.0 %convolution_add_fusion.6 = f32[2048,256]{1,0:T(8,128)S(1)} fusion(f32[512,2048]{1,0:T(8,128)S(1)} %convert_reduce_fusion.10, f32[2048,256]{1,0:T(8,128)S(1)} %get-tuple-element.405, pred[]{:T(512)S(6)} %compare.6, f32[4,512,256]{2,1,0:T(8,128)} %get-tuple-element.415, s32[]{:T(128)S(6)} %copy.78), kind=kOutput, calls=%fused_computation.24.clone.1 | convolution fusion | flops 3222274048 | bytes 8912901 | tf_op jit(solution)/shard_map/while/body/eval_jaxpr/dot_general | solution.py:41
  330.3 3.0 convolution_add_fusion.2
  333.4 4.7 %scatter_custom_fusion = f32[2048,256]{1,0:T(8,128)} fusion(f32[2048,256]{1,0:T(8,128)} %convolution_add_fusion.2, s32[256]{0:T(256)S(1)} %bitcast.123, f32[32,16,256]{2,1,0:T(8,128)S(1)} %convert_element_type.42), kind=kCustom, calls=%fused_computation.53 | custom fusion | flops 65536 | bytes 2359296 | tf_op jit(solution)/shard_map/scatter-add | solution.py:116
  338.1 3.5 %scatter_fusion = f32[2048,256]{1,0:T(8,128)} fusion(f32[2048,256]{1,0:T(8,128)} %scatter_custom_fusion, s32[8]{0:T(128)S(1)} %fusion.26, f32[8,256]{1,0:T(8,128)S(1)} %slice_reduce_fusion), kind=kCustom, calls=%fused_computation.3 | custom fusion | flops 2048 | bytes 24608 | tf_op jit(solution)/shard_map/scatter-add | solution.py:119
  (118 shorter events, 21.4 us)
Async XLA Ops:
  7.2 147.7 %copy-start = (bf16[256,256]{1,0:T(8,128)(2,1)S(1)}, bf16[256,256]{1,0:T(8,128)(2,1)}, u32[]{:S(2)}) copy-start(bf16[256,256]{1,0:T(8,128)(2,1)} %param.18) | copy-start | bytes 393220
  7.2 15.6 %copy-start.7 = (s32[2048]{0:T(1024)S(1)}, s32[2048]{0:T(1024)}, u32[]{:S(2)}) copy-start(s32[2048]{0:T(1024)} %param.22) | copy-start | bytes 24580
  7.2 15.7 %copy-start.5 = (s32[2048,16]{0,1:T(8,128)S(1)}, s32[2048,16]{0,1:T(8,128)}, u32[]{:S(2)}) copy-start(s32[2048,16]{0,1:T(8,128)} %param.21) | copy-start | bytes 393220
  14.5 9.9 %copy-start.1 = (bf16[2048,256]{1,0:T(8,128)(2,1)S(1)}, bf16[2048,256]{1,0:T(8,128)(2,1)}, u32[]{:S(2)}) copy-start(bf16[2048,256]{1,0:T(8,128)(2,1)} %param.16) | copy-start | bytes 3145732
  15.4 105.3 %all-to-all-start = ((bf16[32,16,256]{2,1,0:T(8,128)(2,1)}), bf16[32,16,256]{2,1,0:T(8,128)(2,1)S(1)}, u32[]{:S(2)}, u32[]{:S(2)}) async-start(bf16[32,16,256]{2,1,0:T(8,128)(2,1)} %pad_maximum_fusion), calls=%async_computation | async-start | bytes 524288 | tf_op jit(solution)/shard_map/all_to_all | solution.py:71
  22.8 318.8 %reduce-scatter.2.cloned.1.call-start = ((), (), s32[]{:S(2)}) async-start(), calls=%async_computation.3 | async-start | bytes 540672 | tf_op jit(solution)/shard_map/reduce_scatter | solution.py:121
  154.5 1.6 copy-start.3
  154.5 1.8 copy-start.8
  156.4 3.2 copy-start.2
  158.6 1.0 copy-start.4
  202.3 131.0 %all-to-all-start.1 = ((bf16[32,16,256]{2,1,0:T(8,128)(2,1)}), bf16[32,16,256]{2,1,0:T(8,128)(2,1)S(1)}, u32[]{:S(2)}, u32[]{:S(2)}) async-start(bf16[32,16,256]{2,1,0:T(8,128)(2,1)} %pad_maximum_fusion.2), calls=%async_computation.1 | async-start | bytes 524288 | tf_op jit(solution)/shard_map/all_to_all | solution.py:110
  208.1 122.2 %copy-start.6 = (bf16[256,256]{1,0:T(8,128)(2,1)S(1)}, bf16[256,256]{1,0:T(8,128)(2,1)}, u32[]{:S(2)}) copy-start(bf16[256,256]{1,0:T(8,128)(2,1)} %param.17) | copy-start | bytes 393220
Sparse Core Ops, SparseCore 0:
  164.3 137.1 reduce-scatter.1
where the time goes:
time: 350 us; the launch traced here: 348 us
  other arithmetic  227 us (65%)
  matrix products  71.4 us (20%)
  local copies, waits for them, and re-layouts  22.3 us (6%)
  between operations  14.3 us (4%)
  starting transfers between devices  13.2 us (4%)
    reduce_sum x16, other arithmetic, slot_counts(): return jnp.sum(hits.astype(jnp.float32), axis=1)  212 us
    dot_general x8, matrix products, scatter_one_block(): lax.dot_general(weights, block_weight, (((0,), (0,)), ((), ())), precisio...  48 us
    dot_general x8, matrix products, gather_one_block(): return jnp.dot(weights, source_rows, preferred_element_type=jnp.float32)  10.6 us
    eq x32, local copies, waits for them, and re-layouts, slot_counts(): hits = (index[:, :, None] == columns[None, None, :]) & usable[:, :, None]  8.11 us
    all_to_all x1, starting transfers between devices, body(): lax.all_to_all(packed, 'dom', split_axis=0, concat_axis=0, tiled=True)  7.33 us
  transfers between devices with their start and end apart: 3, of which 0 were waited for; matrix products, arithmetic and copies ran while one was open for 77% of the time, Pallas kernels for 0%

commit v1 on v0

v1 whole, which is shorter than its diff:
```python
import functools

import jax
import jax.numpy as jnp
from jax import lax
from jax.experimental import pallas as pl
from jax.experimental.pallas import tpu as pltpu
from jax.sharding import PartitionSpec as P

LO = 256
BLOCK = 256
BF16 = jnp.bfloat16
F32 = jnp.float32
PARAMS = pltpu.CompilerParams(vmem_limit_bytes=56 * 1024 * 1024)


def dot(a, b, ca, cb):
    return lax.dot_general(a, b, (((ca,), (cb,)), ((), ())), preferred_element_type=F32)


def one_hot_rows(list_column, width):
    lanes = lax.broadcasted_iota(jnp.int32, (list_column.shape[0], width), 1)
    return jnp.where(list_column == lanes, 1.0, 0.0).astype(BF16)


def pack_kernel(lists_ref, features_ref, packed_ref):
    picks = one_hot_rows(lists_ref[...], features_ref.shape[0])
    packed_ref[...] = dot(picks, features_ref[...], 1, 0).astype(BF16)


def count_kernel(local_blocks, index_ref, features_ref, count_ref, summed_ref):
    blocks = count_ref.shape[0]
    groups, lanes = index_ref.shape
    fan = lanes // 16
    rows16 = lax.broadcasted_iota(jnp.int32, (16, lanes), 0)
    cols16 = lax.broadcasted_iota(jnp.int32, (16, lanes), 1) // fan
    own = rows16 == cols16
    low_ids = lax.broadcasted_iota(jnp.int32, (LO, lanes), 0).astype(F32).astype(BF16)
    one = jnp.ones((), BF16)
    zero = jnp.zeros((), BF16)
    for group in range(groups):
        row = index_ref[group : group + 1, :]
        high = jnp.where(own, jnp.broadcast_to(row >> 8, (16, lanes)), -1)
        high = high.astype(F32).astype(BF16)
        low = jnp.broadcast_to((row & (LO - 1)).astype(F32), (16, lanes)).astype(BF16)
        low = jnp.concatenate([low] * (LO // 16), axis=0)
        low_hot = jnp.where(low_ids == low, one, zero)
        high_hot = jnp.concatenate(
            [jnp.where(high == jnp.full((), h, BF16), one, zero) for h in range(blocks)], axis=0
        )
        counted = dot(high_hot, low_hot, 1, 1).astype(BF16)
        for h in range(blocks):
            count_ref[h, 16 * group : 16 * group + 16, :] = counted[16 * h : 16 * h + 16]
    total = jnp.zeros(summed_ref.shape, F32)
    for h in range(local_blocks):
        total = total + dot(count_ref[h], features_ref[h * LO : (h + 1) * LO, :], 1, 0)
    summed_ref[...] = total


def node_kernel(
    summed_ref, count_ref, table_ref, features_ref, cotangent_ref, degree_column_ref,
    degree_row_ref, self_ref, neighbour_ref,
    activations_ref, edge_ref, self_grad_ref, send_ref, weight_ref, send_acc, weight_acc,
):
    step = pl.program_id(0)
    width = features_ref.shape[1]
    remote_blocks = count_ref.shape[0]

    @pl.when(step == 0)
    def _():
        send_acc[...] = jnp.zeros_like(send_acc)
        weight_acc[...] = jnp.zeros_like(weight_acc)

    total = summed_ref[...]
    for h in range(remote_blocks):
        total = total + dot(count_ref[h], table_ref[h * LO : (h + 1) * LO, :], 1, 0)
    mean = (total / degree_column_ref[...]).astype(BF16)
    features = features_ref[...]
    pre = dot(features, self_ref[...], 1, 0) + dot(mean, neighbour_ref[...], 1, 0)
    sig = jax.nn.sigmoid(pre)
    activations_ref[...] = (pre * sig).astype(BF16)
    grad_pre = (cotangent_ref[...].astype(F32) * sig * (1.0 + pre * (1.0 - sig))).astype(BF16)
    edge = (dot(neighbour_ref[...], grad_pre, 1, 1) / degree_row_ref[...]).astype(BF16)
    edge_ref[...] = edge
    self_grad_ref[...] = dot(self_ref[...], grad_pre, 1, 1)
    for h in range(remote_blocks):
        send_acc[:, h * LO : (h + 1) * LO] += dot(edge, count_ref[h], 1, 0)
    weight_acc[:width, :] += dot(features, grad_pre, 0, 0)
    weight_acc[width:, :] += dot(mean, grad_pre, 0, 0)

    @pl.when(step == pl.num_programs(0) - 1)
    def _():
        send_ref[...] = send_acc[...].T.astype(BF16)
        weight_ref[...] = weight_acc[...].astype(BF16)


def local_kernel(count_ref, edge_ref, self_grad_ref, out_ref):
    out_ref[...] = self_grad_ref[...] + dot(edge_ref[...], count_ref[0], 1, 0)


def final_kernel(part_ref, lists_ref, returned_ref, out_ref):
    nodes = out_ref.shape[0]
    lanes = lax.broadcasted_iota(jnp.int32, (lists_ref.shape[0], nodes), 1)
    lanes = lanes + pl.program_id(0) * nodes
    picks = jnp.where(lists_ref[...] == lanes, 1.0, 0.0).astype(BF16)
    out_ref[...] = (part_ref[...] + dot(returned_ref[...], picks, 0, 0)).T


def body(
    features, self_weight, neighbour_weight, send_lists, hub_nodes, neighbours, counts, cotangent
):
    nodes, width = features.shape
    fan = neighbours.shape[1]
    peers = lax.axis_size("dom")
    per_peer = send_lists.shape[2]
    hubs = hub_nodes.shape[1]
    both = per_peer + hubs
    remote = peers * both
    local_blocks = nodes // LO
    blocks = local_blocks + remote // LO
    remote_blocks = blocks - local_blocks
    steps = nodes // BLOCK

    lists = jnp.concatenate(
        [send_lists[0], jnp.broadcast_to(hub_nodes, (peers, hubs))], axis=1
    ).reshape(remote, 1)
    packed = pl.pallas_call(
        pack_kernel,
        out_shape=jax.ShapeDtypeStruct((remote, width), BF16),
        compiler_params=PARAMS,
        name="pack",
    )(lists, features)
    arrived = lax.all_to_all(
        packed.reshape(peers, both, width), "dom", split_axis=0, concat_axis=0, tiled=True
    ).reshape(remote, width)

    past = neighbours - nodes
    hub_past = past - peers * per_peer
    remapped = jnp.where(
        past < 0,
        neighbours,
        nodes
        + jnp.where(
            hub_past < 0,
            (past // per_peer) * both + past % per_peer,
            (hub_past // hubs) * both + per_peer + hub_past % hubs,
        ),
    )
    usable = jnp.arange(fan, dtype=jnp.int32)[None, :] < counts[:, None]
    index = jnp.where(usable, remapped, -1).reshape(nodes // 16, 16 * fan)

    count, summed = pl.pallas_call(
        functools.partial(count_kernel, local_blocks),
        grid=(steps,),
        in_specs=[
            pl.BlockSpec((BLOCK // 16, 16 * fan), lambda i: (i, 0)),
            pl.BlockSpec((nodes, width), lambda i: (0, 0)),
        ],
        out_specs=[
            pl.BlockSpec((blocks, BLOCK, LO), lambda i: (0, i, 0)),
            pl.BlockSpec((BLOCK, width), lambda i: (i, 0)),
        ],
        out_shape=[
            jax.ShapeDtypeStruct((blocks, nodes, LO), BF16),
            jax.ShapeDtypeStruct((nodes, width), F32),
        ],
        compiler_params=PARAMS,
        cost_estimate=pl.CostEstimate(
            flops=4 * nodes * blocks * LO * width, bytes_accessed=16 << 20, transcendentals=0
        ),
        name="count",
    )(index, features)

    degree = counts.astype(F32)
    whole = lambda i: (0, 0)
    activations, edge, self_grad, send, weight = pl.pallas_call(
        node_kernel,
        grid=(steps,),
        in_specs=[
            pl.BlockSpec((BLOCK, width), lambda i: (i, 0)),
            pl.BlockSpec(
                (remote_blocks, BLOCK, LO), lambda i: (local_blocks // remote_blocks, i, 0)
            ),
            pl.BlockSpec((remote, width), whole),
            pl.BlockSpec((BLOCK, width), lambda i: (i, 0)),
            pl.BlockSpec((BLOCK, width), lambda i: (i, 0)),
            pl.BlockSpec((BLOCK, 1), lambda i: (i, 0)),
            pl.BlockSpec((1, BLOCK), lambda i: (0, i)),
            pl.BlockSpec((width, width), whole),
            pl.BlockSpec((width, width), whole),
        ],
        out_specs=[
            pl.BlockSpec((BLOCK, width), lambda i: (i, 0)),
            pl.BlockSpec((width, BLOCK), lambda i: (0, i)),
            pl.BlockSpec((width, BLOCK), lambda i: (0, i)),
            pl.BlockSpec((remote, width), whole),
            pl.BlockSpec((2 * width, width), whole),
        ],
        out_shape=[
            jax.ShapeDtypeStruct((nodes, width), BF16),
            jax.ShapeDtypeStruct((width, nodes), BF16),
            jax.ShapeDtypeStruct((width, nodes), F32),
            jax.ShapeDtypeStruct((remote, width), BF16),
            jax.ShapeDtypeStruct((2 * width, width), BF16),
        ],
        scratch_shapes=[
            pltpu.VMEM((width, remote), F32),
            pltpu.VMEM((2 * width, width), F32),
        ],
        compiler_params=PARAMS,
        name="node",
    )(
        summed, count, arrived, features, cotangent, degree[:, None], degree[None, :],
        self_weight, neighbour_weight,
    )
    outgoing = jnp.concatenate(
        [send.reshape(peers, both, width), weight.reshape(peers, 2 * width // peers, width)],
        axis=1,
    )
    returned = lax.all_to_all(outgoing, "dom", split_axis=0, concat_axis=0, tiled=True)

    part = pl.pallas_call(
        local_kernel,
        grid=(local_blocks,),
        in_specs=[
            pl.BlockSpec((1, nodes, LO), lambda h: (h, 0, 0)),
            pl.BlockSpec((width, nodes), whole),
            pl.BlockSpec((width, LO), lambda h: (0, h)),
        ],
        out_specs=pl.BlockSpec((width, LO), lambda h: (0, h)),
        out_shape=jax.ShapeDtypeStruct((width, nodes), F32),
        compiler_params=PARAMS,
        cost_estimate=pl.CostEstimate(
            flops=2 * nodes * nodes * width, bytes_accessed=12 << 20, transcendentals=0
        ),
        name="local",
    )(count, edge, self_grad)

    grad_features = pl.pallas_call(
        final_kernel,
        grid=(nodes // 512,),
        in_specs=[
            pl.BlockSpec((width, 512), lambda i: (0, i)),
            pl.BlockSpec((remote, 1), whole),
            pl.BlockSpec((remote, width), whole),
        ],
        out_specs=pl.BlockSpec((512, width), lambda i: (i, 0)),
        out_shape=jax.ShapeDtypeStruct((nodes, width), F32),
        compiler_params=PARAMS,
        name="final",
    )(part, lists, returned[:, :both].reshape(remote, width))
    grad_weights = jnp.sum(returned[:, both:].astype(F32), axis=0)
    return (activations, grad_features, grad_weights)


def solution(mesh):
    in_specs = (
        P("dom", None),
        P(),
        P(),
        P("dom", None, None),
        P("dom", None),
        P("dom", None),
        P("dom"),
        P("dom", None),
    )
    out_specs = (P("dom", None), P("dom", None), P("dom", None))
    return jax.shard_map(body, mesh=mesh, in_specs=in_specs, out_specs=out_specs, check_vma=False)
```

time: 350 us -> 74.3 us (0.21)
  other arithmetic: 227 us -> 3.57 us
  matrix products: 71.4 us -> 0 us
  Pallas kernels: 0 us -> 43.6 us
  local copies, waits for them, and re-layouts: 22.3 us -> 5.96 us
  between operations: 14.3 us -> 0.73 us
  waiting for transfers between devices: 0.02 us -> 6.44 us
    reduce_sum x17 -> x1, other arithmetic: 212 us -> 0.65 us  [body(): grad_weights = jnp.sum(returned[:, both:].astype(F32), axis=0)]
    dot_general x21 -> x0, matrix products: 71.4 us -> none  [the longest x8 48 us: scatter_one_block(): lax.dot_general(weights, block_weight, (((0,), (0,)), ((), ())), precisio...]
    pallas_call x0 -> x5, Pallas kernels: none -> 43.6 us  [the longest x1 15.4 us: body(): pl.pallas_call(functools.partial(count_kernel, local_blocks), grid=(steps...]
    scatter-add x2 -> x0, other arithmetic: 8.19 us -> none  [the longest x1 4.7 us: body(): grad_features.at[lists_flat]]
    eq x32 -> x0, local copies, waits for them, and re-layouts: 8.11 us -> none  [slot_counts(): hits = (index[:, :, None] == columns[None, None, :]) & usable[:, :, None]]
    all_to_all x2, waiting for transfers between devices: 0.01 us -> 6.44 us  [the longest x1 6.44 us: body(): lax.all_to_all(outgoing, 'dom', split_axis=0, concat_axis=0, tiled=True)]
    gather x2 -> x0, local copies, waits for them, and re-layouts: 4.25 us -> none  [the longest x1 2.33 us: body(): jnp.take(features, lists_flat, axis=0)]
  transfers between devices with their start and end apart: 3 -> 2, of which waited for: 0 -> 1; matrix products, arithmetic and copies ran while one was open for 77% -> 4% of each run, Pallas kernels for 0% -> 33%
where the time goes in v1:
time: 74.3 us; the launch traced here: 73.5 us
  Pallas kernels  43.6 us (59%)
  starting transfers between devices  13.2 us (18%)
  waiting for transfers between devices  6.44 us (9%)
  local copies, waits for them, and re-layouts  5.96 us (8%)
  other arithmetic  3.57 us (5%)
    pallas_call x1, Pallas kernels, body(): pl.pallas_call(functools.partial(count_kernel, local_blocks), grid=(steps...  15.4 us
    pallas_call x1, Pallas kernels, body(): pl.pallas_call(node_kernel, grid=(steps,), in_specs=[pl.BlockSpec((BLOCK,...  11.4 us
    pallas_call x1, Pallas kernels, body(): pl.pallas_call(local_kernel, grid=(local_blocks,), in_specs=[pl.BlockSpec...  9.17 us
    all_to_all x1, starting transfers between devices, body(): lax.all_to_all(packed.reshape(peers, both, width), 'dom', split_axis=0, c...  7.33 us
    all_to_all x1, waiting for transfers between devices, body(): lax.all_to_all(outgoing, 'dom', split_axis=0, concat_axis=0, tiled=True)  6.44 us
    all_to_all x1, starting transfers between devices, body(): lax.all_to_all(outgoing, 'dom', split_axis=0, concat_axis=0, tiled=True)  5.83 us
    pallas_call x1, Pallas kernels, body(): pl.pallas_call(final_kernel, grid=(nodes // 512,), in_specs=[pl.BlockSpec...  4.93 us
    pallas_call x1, Pallas kernels, body(): pl.pallas_call(pack_kernel, out_shape=jax.ShapeDtypeStruct((remote, width...  2.77 us
  transfers between devices with their start and end apart: 2, of which 1 were waited for; matrix products, arithmetic and copies ran while one was open for 4% of the time, Pallas kernels for 33%

profile of v1, /device:TPU:0, one launch (start us, length us, event | category | flops | bytes accessed | tf_op | source)
XLA Modules:
  0.0 73.5 jit_solution(9077888988311419685)
XLA Ops:
  0.6 0.0 copy-start.3
  0.6 0.0 copy-start.1
  0.7 0.8 %pad.3.clone = s32[16]{0:T(128)S(1)} pad(s32[8]{0:T(128)} %bitcast.17, s32[]{:T(128)} %constant.45.clone.1), padding=8_0 | pad | bytes 100 | tf_op jit(solution)/shard_map/concatenate | solution.py:124
  1.4 0.8 %pad_add_fusion = s32[32,16]{0,1:T(8,128)S(1)} fusion(s32[32,8]{0,1:T(8,128)} %bitcast.16, s32[16]{0:T(128)S(1)} %pad.3.clone), kind=kLoop, calls=%fused_computation.32 | loop fusion | flops 512 | bytes 3136 | tf_op jit(solution)/shard_map/concatenate | solution.py:124
  2.2 0.1 copy.14
  2.3 0.9 %reshape.35.lists_ref = s32[512,1]{1,0:T(8,128)} reshape(s32[32,16]{1,0:T(8,128)S(1)} %copy.14) | data formatting | bytes 4096 | tf_op jit(solution)/shard_map/reshape | solution.py:126
  3.1 2.8 %pack.1 = bf16[512,256]{1,0:T(8,128)(2,1)} custom-call(s32[512,1]{1,0:T(8,128)} %reshape.35.lists_ref, bf16[2048,256]{1,0:T(8,128)(2,1)} %features_ref.5), custom_call_target="tpu_custom_call" | custom-call | tf_op jit(solution)/shard_map/pack/pallas_call | solution.py:127
  5.9 7.3 %all-to-all-start = ((bf16[32,16,256]{2,1,0:T(8,128)(2,1)}), bf16[32,16,256]{2,1,0:T(8,128)(2,1)S(1)}, u32[]{:S(2)}, u32[]{:S(2)}) async-start(bf16[32,16,256]{2,1,0:T(8,128)(2,1)} %bitcast.11), calls=%async_computation | async-start | bytes 524288 | tf_op jit(solution)/shard_map/all_to_all | solution.py:133
  13.2 0.0 copy-done.3
  13.2 0.0 copy-done.1
  13.2 0.3 fusion.5
  13.5 0.0 copy-start.2
  13.6 0.3 copy.13
  13.9 1.1 %reshape.28.index_ref = s32[128,256]{1,0:T(8,128)} reshape(s32[2048,16]{1,0:T(8,128)S(1)} %copy.13) | data formatting | bytes 262144 | tf_op jit(solution)/shard_map/reshape | solution.py:150
  14.9 1.4 %copy.16.degree_column_ref = f32[2048,1]{1,0:T(8,128)} copy(f32[2048,1]{0,1:T(1,128)S(1)} %bitcast.14) | data formatting | bytes 16384 | tf_op jit(solution)/shard_map/broadcast_in_dim | solution.py:213
  16.4 15.4 %count.1 = (bf16[10,2048,256]{2,1,0:T(8,128)(2,1)}, f32[2048,256]{1,0:T(8,128)}) custom-call(s32[128,256]{1,0:T(8,128)} %reshape.28.index_ref, bf16[2048,256]{1,0:T(8,128)(2,1)} %features_ref.5), custom_call_target="tpu_custom_call" | custom-call | flops 5368709120 | bytes 16777216 | tf_op jit(solution)/shard_map/count/pallas_call | solution.py:152
  31.7 0.0 copy-done.2
  31.7 0.0 all-to-all-done
  31.7 0.0 copy-start
  31.7 0.7 copy-done
  32.4 11.4 %node.1 = (bf16[2048,256]{1,0:T(8,128)(2,1)}, bf16[256,2048]{1,0:T(8,128)(2,1)}, f32[256,2048]{1,0:T(8,128)}, bf16[512,256]{1,0:T(8,128)(2,1)}, bf16[512,256]{1,0:T(8,128)(2,1)}) custom-call(f32[2048,256]{1,0:T(8,128)} %get-tuple-element.10.summed_ref, bf16[10,2048,256]{2,1,0:T(8,128)(2,1)} %get-tuple-element.11.count_ref, bf16[512,256]{1,0:T(8,128)(2,1)} %bitcast.9, ...), custom_call_target="tpu_custom_call" | custom-call | tf_op jit(solution)/shard_map/node/pallas_call | solution.py:176
  43.8 1.9 %pad_maximum_fusion = bf16[32,32,256]{2,1,0:T(8,128)(2,1)} fusion(bf16[32,16,256]{2,1,0:T(8,128)(2,1)} %bitcast.13, bf16[32,16,256]{2,1,0:T(8,128)(2,1)} %bitcast.12), kind=kLoop, calls=%fused_computation | loop fusion | flops 1048576 | bytes 1048576 | tf_op jit(solution)/shard_map/concatenate | solution.py:216
  45.7 5.8 %all-to-all-start.1 = ((bf16[32,32,256]{2,1,0:T(8,128)(2,1)}), bf16[32,32,256]{2,1,0:T(8,128)(2,1)S(1)}, u32[]{:S(2)}, u32[]{:S(2)}) async-start(bf16[32,32,256]{2,1,0:T(8,128)(2,1)} %pad_maximum_fusion), calls=%async_computation.1 | async-start | bytes 1048576 | tf_op jit(solution)/shard_map/all_to_all | solution.py:220
  51.5 9.2 %local.1.part_ref = f32[256,2048]{1,0:T(8,128)} custom-call(bf16[10,2048,256]{2,1,0:T(8,128)(2,1)} %get-tuple-element.11.count_ref, bf16[256,2048]{1,0:T(8,128)(2,1)} %get-tuple-element.13.edge_ref, f32[256,2048]{1,0:T(8,128)} %get-tuple-element.14.self_grad_ref), custom_call_target="tpu_custom_call" | custom-call | flops 2147483648 | bytes 12582912 | tf_op jit(solution)/shard_map/local/pallas_call | solution.py:222
  60.7 6.4 %all-to-all-done.1 = bf16[32,32,256]{2,1,0:T(8,128)(2,1)S(1)} async-done(((bf16[32,32,256]{2,1,0:T(8,128)(2,1)}), bf16[32,32,256]{2,1,0:T(8,128)(2,1)S(1)}, u32[]{:S(2)}, u32[]{:S(2)}) %all-to-all-start.1) | async-done | bytes 524320 | tf_op jit(solution)/shard_map/all_to_all | solution.py:220
  67.2 0.7 %slice.8 = bf16[32,16,256]{2,1,0:T(8,128)(2,1)} slice(bf16[32,32,256]{2,1,0:T(8,128)(2,1)S(1)} %all-to-all-done.1), slice={[0:32], [0:16], [0:256]} | slice | bytes 524288 | tf_op jit(solution)/shard_map/slice | solution.py:251
  67.9 4.9 %final.1 = f32[2048,256]{1,0:T(8,128)} custom-call(f32[256,2048]{1,0:T(8,128)} %local.1.part_ref, s32[512,1]{1,0:T(8,128)} %reshape.35.lists_ref, bf16[512,256]{1,0:T(8,128)(2,1)} %bitcast.10), custom_call_target="tpu_custom_call" | custom-call | tf_op jit(solution)/shard_map/final/pallas_call | solution.py:239
  72.8 0.7 convert_reduce_fusion
  (1 shorter events, 0.0 us)
Async XLA Ops:
  0.6 12.6 %copy-start.3 = (s32[2048]{0:T(1024)S(1)}, s32[2048]{0:T(1024)}, u32[]{:S(2)}) copy-start(s32[2048]{0:T(1024)} %param.14) | copy-start | bytes 24580
  0.6 12.6 %copy-start.1 = (s32[2048,16]{0,1:T(8,128)S(1)}, s32[2048,16]{0,1:T(8,128)}, u32[]{:S(2)}) copy-start(s32[2048,16]{0,1:T(8,128)} %param.13) | copy-start | bytes 393220
  5.9 25.8 %all-to-all-start = ((bf16[32,16,256]{2,1,0:T(8,128)(2,1)}), bf16[32,16,256]{2,1,0:T(8,128)(2,1)S(1)}, u32[]{:S(2)}, u32[]{:S(2)}) async-start(bf16[32,16,256]{2,1,0:T(8,128)(2,1)} %bitcast.11), calls=%async_computation | async-start | bytes 524288 | tf_op jit(solution)/shard_map/all_to_all | solution.py:133
  13.5 18.2 %copy-start.2 = (f32[2048]{0:T(1024)}, f32[2048]{0:T(1024)S(1)}, u32[]{:S(2)}) copy-start(f32[2048]{0:T(1024)S(1)} %convert_element_type.6) | copy-start | bytes 24580
  31.7 0.7 copy-start
  45.7 21.5 %all-to-all-start.1 = ((bf16[32,32,256]{2,1,0:T(8,128)(2,1)}), bf16[32,32,256]{2,1,0:T(8,128)(2,1)S(1)}, u32[]{:S(2)}, u32[]{:S(2)}) async-start(bf16[32,32,256]{2,1,0:T(8,128)(2,1)} %pad_maximum_fusion), calls=%async_computation.1 | async-start | bytes 1048576 | tf_op jit(solution)/shard_map/all_to_all | solution.py:220

commit v2 on v0

v2 whole, which is shorter than its diff:
```python
import functools

import jax
import jax.numpy as jnp
from jax import lax
from jax.experimental import pallas as pl
from jax.experimental.pallas import tpu as pltpu
from jax.sharding import PartitionSpec as P

LO = 256
BLOCK = 256
BF16 = jnp.bfloat16
F32 = jnp.float32
MESH = pl.DeviceIdType.MESH


def dot(a, b, ca, cb):
    return lax.dot_general(a, b, (((ca,), (cb,)), ((), ())), preferred_element_type=F32)


def whole_kernel(
    peers,
    index_ref, lists_ref, degree_column_ref, degree_row_ref, features_ref, cotangent_ref,
    self_ref, neighbour_ref,
    activations_ref, out_ref, weight_out_ref,
    packed, table, count, summed, edge, part, mean_all, pre_grad, send, returned,
    weight_acc, weight_send, weight_in,
    send_sem, recv_sem, back_send_sem, back_recv_sem, weight_send_sem, weight_recv_sem,
):
    me = lax.axis_index("dom")
    nodes, width = features_ref.shape
    remote = packed.shape[0]
    both = remote // peers
    blocks = count.shape[0]
    local_blocks = nodes // LO
    remote_blocks = blocks - local_blocks
    lanes = index_ref.shape[1]
    fan = lanes // 16
    share = weight_send.shape[1]
    own = pl.ds(pl.multiple_of(me * both, both), both)

    barrier = pltpu.get_barrier_semaphore()

    @pl.loop(1, peers)
    def _(p):
        pl.semaphore_signal(
            barrier, inc=1, device_id=(lax.rem(me + p, peers),), device_id_type=MESH
        )

    for start in range(0, remote, 512):
        rows = lists_ref[start : start + 512, :]
        ids = lax.broadcasted_iota(jnp.int32, (512, nodes), 1)
        picks = jnp.where(rows == ids, 1.0, 0.0).astype(BF16)
        packed[start : start + 512, :] = dot(picks, features_ref[...], 1, 0).astype(BF16)
    table[own, :] = packed[own, :]
    pl.semaphore_wait(barrier, peers - 1)

    @pl.loop(1, peers)
    def _(p):
        peer = lax.rem(me + p, peers)
        pltpu.make_async_remote_copy(
            src_ref=packed.at[pl.ds(pl.multiple_of(peer * both, both), both)],
            dst_ref=table.at[own],
            send_sem=send_sem,
            recv_sem=recv_sem,
            device_id=(peer,),
            device_id_type=MESH,
        ).start()

    rows16 = lax.broadcasted_iota(jnp.int32, (16, lanes), 0)
    cols16 = lax.broadcasted_iota(jnp.int32, (16, lanes), 1) // fan
    mine = rows16 == cols16
    low_ids = lax.broadcasted_iota(jnp.int32, (LO, lanes), 0).astype(F32).astype(BF16)
    one = jnp.ones((), BF16)
    zero = jnp.zeros((), BF16)

    @pl.loop(0, nodes // BLOCK)
    def _(step):
        groups = BLOCK // 16
        index = index_ref[pl.ds(pl.multiple_of(step * groups, groups), groups), :]
        for group in range(groups):
            row = index[group : group + 1, :]
            high = jnp.where(mine, jnp.broadcast_to(row >> 8, (16, lanes)), -1)
            high = high.astype(F32).astype(BF16)
            low = jnp.broadcast_to((row & (LO - 1)).astype(F32), (16, lanes)).astype(BF16)
            low = jnp.concatenate([low] * (LO // 16), axis=0)
            low_hot = jnp.where(low_ids == low, one, zero)
            high_hot = jnp.concatenate(
                [jnp.where(high == jnp.full((), h, BF16), one, zero) for h in range(blocks)],
                axis=0,
            )
            counted = dot(high_hot, low_hot, 1, 1).astype(BF16)
            at = pl.ds(pl.multiple_of(step * BLOCK + 16 * group, 16), 16)
            for h in range(blocks):
                count[h, at, :] = counted[16 * h : 16 * h + 16]
        at = pl.ds(pl.multiple_of(step * BLOCK, BLOCK), BLOCK)
        total = jnp.zeros((BLOCK, width), F32)
        for h in range(local_blocks):
            total = total + dot(count[h, at, :], features_ref[h * LO : (h + 1) * LO, :], 1, 0)
        summed[at, :] = total

    others = pl.ds(0, (peers - 1) * both)
    pltpu.make_async_copy(table.at[others], table.at[others], recv_sem).wait()

    @pl.loop(0, nodes // BLOCK)
    def _(step):
        at = pl.ds(pl.multiple_of(step * BLOCK, BLOCK), BLOCK)
        total = summed[at, :]
        for h in range(remote_blocks):
            total = total + dot(
                count[local_blocks + h, at, :], table[h * LO : (h + 1) * LO, :], 1, 0
            )
        mean = (total / degree_column_ref[at, :]).astype(BF16)
        mean_all[at, :] = mean
        pre = dot(features_ref[at, :], self_ref[...], 1, 0) + dot(mean, neighbour_ref[...], 1, 0)
        sig = jax.nn.sigmoid(pre)
        activations_ref[at, :] = (pre * sig).astype(BF16)
        grad_pre = (
            cotangent_ref[at, :].astype(F32) * sig * (1.0 + pre * (1.0 - sig))
        ).astype(BF16)
        pre_grad[at, :] = grad_pre
        edge[:, at] = (dot(neighbour_ref[...], grad_pre, 1, 1) / degree_row_ref[:, at]).astype(BF16)
        part[:, at] = dot(self_ref[...], grad_pre, 1, 1)

    for h in range(remote_blocks):
        send[h * LO : (h + 1) * LO, :] = dot(edge[...], count[local_blocks + h], 1, 0).T.astype(BF16)
    returned[own, :] = send[own, :]

    @pl.loop(1, peers)
    def _(p):
        peer = lax.rem(me + p, peers)
        pltpu.make_async_remote_copy(
            src_ref=send.at[pl.ds(pl.multiple_of(peer * both, both), both)],
            dst_ref=returned.at[own],
            send_sem=back_send_sem,
            recv_sem=back_recv_sem,
            device_id=(peer,),
            device_id_type=MESH,
        ).start()

    weight_acc[:width, :] = dot(features_ref[...], pre_grad[...], 0, 0)
    weight_acc[width:, :] = dot(mean_all[...], pre_grad[...], 0, 0)
    for p in range(peers):
        weight_send[p] = weight_acc[p * share : (p + 1) * share, :].astype(BF16)
    weight_in[me] = weight_send[me]

    @pl.loop(1, peers)
    def _(p):
        peer = lax.rem(me + p, peers)
        pltpu.make_async_remote_copy(
            src_ref=weight_send.at[peer],
            dst_ref=weight_in.at[me],
            send_sem=weight_send_sem,
            recv_sem=weight_recv_sem,
            device_id=(peer,),
            device_id_type=MESH,
        ).start()

    @pl.loop(0, local_blocks)
    def _(h):
        at = pl.ds(pl.multiple_of(h * LO, LO), LO)
        part[:, at] = part[:, at] + dot(edge[...], count[h], 1, 0)

    pltpu.make_async_copy(returned.at[others], returned.at[others], back_recv_sem).wait()

    @pl.loop(0, nodes // BLOCK)
    def _(step):
        at = pl.ds(pl.multiple_of(step * BLOCK, BLOCK), BLOCK)
        ids = lax.broadcasted_iota(jnp.int32, (remote, BLOCK), 1) + step * BLOCK
        picks = jnp.where(lists_ref[...] == ids, 1.0, 0.0).astype(BF16)
        out_ref[at, :] = (part[:, at] + dot(returned[...], picks, 0, 0)).T

    rest = pl.ds(0, peers - 1)
    pltpu.make_async_copy(weight_in.at[rest], weight_in.at[rest], weight_recv_sem).wait()
    weight_out_ref[...] = jnp.sum(weight_in[...].astype(F32), axis=0)
    pltpu.make_async_copy(packed.at[others], packed.at[others], send_sem).wait()
    pltpu.make_async_copy(send.at[others], send.at[others], back_send_sem).wait()
    pltpu.make_async_copy(weight_send.at[rest], weight_send.at[rest], weight_send_sem).wait()


def body(
    features, self_weight, neighbour_weight, send_lists, hub_nodes, neighbours, counts, cotangent
):
    nodes, width = features.shape
    fan = neighbours.shape[1]
    peers = lax.axis_size("dom")
    per_peer = send_lists.shape[2]
    hubs = hub_nodes.shape[1]
    both = per_peer + hubs
    remote = peers * both
    blocks = (nodes + remote) // LO
    share = 2 * width // peers

    lists = jnp.concatenate(
        [send_lists[0], jnp.broadcast_to(hub_nodes, (peers, hubs))], axis=1
    ).reshape(remote, 1)
    past = neighbours - nodes
    hub_past = past - peers * per_peer
    remapped = jnp.where(
        past < 0,
        neighbours,
        nodes
        + jnp.where(
            hub_past < 0,
            (past // per_peer) * both + past % per_peer,
            (hub_past // hubs) * both + per_peer + hub_past % hubs,
        ),
    )
    usable = jnp.arange(fan, dtype=jnp.int32)[None, :] < counts[:, None]
    index = jnp.where(usable, remapped, -1).reshape(nodes // 16, 16 * fan)
    degree = counts.astype(F32)
    vmem = pl.BlockSpec(memory_space=pltpu.VMEM)
    return pl.pallas_call(
        functools.partial(whole_kernel, peers),
        in_specs=[vmem] * 8,
        out_specs=[vmem] * 3,
        out_shape=[
            jax.ShapeDtypeStruct((nodes, width), BF16),
            jax.ShapeDtypeStruct((nodes, width), F32),
            jax.ShapeDtypeStruct((share, width), F32),
        ],
        scratch_shapes=[
            pltpu.VMEM((remote, width), BF16),
            pltpu.VMEM((remote, width), BF16),
            pltpu.VMEM((blocks, nodes, LO), BF16),
            pltpu.VMEM((nodes, width), F32),
            pltpu.VMEM((width, nodes), BF16),
            pltpu.VMEM((width, nodes), F32),
            pltpu.VMEM((nodes, width), BF16),
            pltpu.VMEM((nodes, width), BF16),
            pltpu.VMEM((remote, width), BF16),
            pltpu.VMEM((remote, width), BF16),
            pltpu.VMEM((2 * width, width), F32),
            pltpu.VMEM((peers, share, width), BF16),
            pltpu.VMEM((peers, share, width), BF16),
        ]
        + [pltpu.SemaphoreType.DMA] * 6,
        compiler_params=pltpu.CompilerParams(
            collective_id=0, has_side_effects=True, vmem_limit_bytes=60 * 1024 * 1024
        ),
        name="whole",
    )(
        index, lists, degree[:, None], degree[None, :], features, cotangent, self_weight,
        neighbour_weight,
    )


def solution(mesh):
    in_specs = (
        P("dom", None),
        P(),
        P(),
        P("dom", None, None),
        P("dom", None),
        P("dom", None),
        P("dom"),
        P("dom", None),
    )
    out_specs = (P("dom", None), P("dom", None), P("dom", None))
    return jax.shard_map(body, mesh=mesh, in_specs=in_specs, out_specs=out_specs, check_vma=False)
```

time: 350 us -> 54.2 us (0.15)
  other arithmetic: 227 us -> 2.64 us
  matrix products: 71.4 us -> 0 us
  Pallas kernels: 0 us -> 41.3 us
  between operations: 14.3 us -> 0.66 us
  local copies, waits for them, and re-layouts: 22.3 us -> 8.74 us
  starting transfers between devices: 13.2 us -> 0 us
    reduce_sum x17 -> x0, other arithmetic: 212 us -> none  [the longest x16 212 us: slot_counts(): return jnp.sum(hits.astype(jnp.float32), axis=1)]
    dot_general x21 -> x0, matrix products: 71.4 us -> none  [the longest x8 48 us: scatter_one_block(): lax.dot_general(weights, block_weight, (((0,), (0,)), ((), ())), precisio...]
    pallas_call x0 -> x1, Pallas kernels: none -> 41.3 us  [body(): pl.pallas_call(functools.partial(whole_kernel, peers), in_specs=[vmem] *...]
    all_to_all x2 -> x0, starting transfers between devices: 13.2 us -> none  [the longest x1 7.33 us: body(): lax.all_to_all(packed, 'dom', split_axis=0, concat_axis=0, tiled=True)]
    scatter-add x2 -> x0, other arithmetic: 8.19 us -> none  [the longest x1 4.7 us: body(): grad_features.at[lists_flat]]
    eq x32 -> x0, local copies, waits for them, and re-layouts: 8.11 us -> none  [slot_counts(): hits = (index[:, :, None] == columns[None, None, :]) & usable[:, :, None]]
    gather x2 -> x0, local copies, waits for them, and re-layouts: 4.25 us -> none  [the longest x1 2.33 us: body(): jnp.take(features, lists_flat, axis=0)]
  transfers between devices with their start and end apart: 3 -> 0, of which waited for: 0 -> 0; matrix products, arithmetic and copies ran while one was open for 77% -> 0% of each run, Pallas kernels for 0% -> 0%
where the time goes in v2:
time: 54.2 us; the launch traced here: 53.4 us
  Pallas kernels  41.3 us (76%)
  local copies, waits for them, and re-layouts  8.74 us (16%)
  other arithmetic  2.64 us (5%)
  between operations  0.66 us (1%)
    pallas_call x1, Pallas kernels, body(): pl.pallas_call(functools.partial(whole_kernel, peers), in_specs=[vmem] *...  41.3 us
    unnamed x9, local copies, waits for them, and re-layouts  4.35 us
    broadcast_in_dim x1, local copies, waits for them, and re-layouts, body(): degree[:, None]  1.34 us
    select_n x1, other arithmetic, body(): index = jnp.where(usable, remapped, -1).reshape(nodes // 16, 16 * fan)  1.18 us

profile of v2, /device:TPU:0, one launch (start us, length us, event | category | flops | bytes accessed | tf_op | source)
XLA Modules:
  0.0 53.4 jit_solution(12660293042814180844)
XLA Ops:
  0.6 0.7 %pad.1.clone = s32[16]{0:T(128)S(1)} pad(s32[8]{0:T(128)} %bitcast.7, s32[]{:T(128)} %constant.44.clone.1), padding=8_0 | pad | bytes 100 | tf_op jit(solution)/shard_map/concatenate | solution.py:194
  1.4 0.8 %pad_add_fusion = s32[32,16]{0,1:T(8,128)S(1)} fusion(s32[32,8]{0,1:T(8,128)} %bitcast.6, s32[16]{0:T(128)S(1)} %pad.1.clone), kind=kLoop, calls=%fused_computation.30 | loop fusion | flops 512 | bytes 3136 | tf_op jit(solution)/shard_map/concatenate | solution.py:194
  2.1 0.7 %convert_element_type.3 = f32[2048]{0:T(1024)S(1)} convert(s32[2048]{0:T(1024)} %param.14) | non-fusion elementwise | flops 2048 | bytes 16384 | tf_op jit(solution)/shard_map/convert_element_type | solution.py:211
  2.8 0.0 copy-start.1
  2.8 0.1 copy.14
  2.9 1.2 %fusion.5 = s32[2048,16]{0,1:T(8,128)S(1)} fusion(s32[2048,16]{0,1:T(8,128)} %param.13, s32[2048]{0:T(1024)} %param.14), kind=kLoop, calls=%fused_computation.15 | loop fusion | flops 1638400 | bytes 270336 | tf_op jit(solution)/shard_map/jit(_where)/select_n | solution.py:210
  4.1 0.9 %reshape.15.lists_ref = s32[512,1]{1,0:T(8,128)} reshape(s32[32,16]{1,0:T(8,128)S(1)} %copy.14) | data formatting | bytes 4096 | tf_op jit(solution)/shard_map/reshape | solution.py:196
  4.9 0.3 copy.13
  5.3 1.1 %reshape.13.index_ref = s32[128,256]{1,0:T(8,128)} reshape(s32[2048,16]{1,0:T(8,128)S(1)} %copy.13) | data formatting | bytes 262144 | tf_op jit(solution)/shard_map/reshape | solution.py:210
  6.3 1.3 %copy.16.degree_column_ref = f32[2048,1]{1,0:T(8,128)} copy(f32[2048,1]{0,1:T(1,128)S(1)} %bitcast.4) | data formatting | bytes 16384 | tf_op jit(solution)/shard_map/broadcast_in_dim | solution.py:243
  7.7 0.0 copy-done.1
  7.7 41.3 %whole.1 = (bf16[2048,256]{1,0:T(8,128)(2,1)}, f32[2048,256]{1,0:T(8,128)}, f32[16,256]{1,0:T(8,128)}) custom-call(s32[128,256]{1,0:T(8,128)} %reshape.13.index_ref, s32[512,1]{1,0:T(8,128)} %reshape.15.lists_ref, f32[2048,1]{1,0:T(8,128)} %copy.16.degree_column_ref, f32[1,2048]{1,0:T(1,128)} %bitcast.5, bf16[2048,256]{1,0:T(8,128)(2,1)} %features_ref.1, ...), custom_call_target="tpu_custom_call" | custom-call | tf_op jit(solution)/shard_map/whole/pallas_call | solution.py:213
  49.0 0.0 copy-start
  49.0 2.4 %copy.20 = bf16[2048,256]{1,0:T(8,128)(2,1)} copy(bf16[2048,256]{1,0:T(8,128)(2,1)} %get-tuple-element.6) | data formatting | bytes 2097152
  51.4 0.0 copy-done
  51.4 0.0 copy-start.2
  51.4 1.3 %copy.21 = f32[2048,256]{1,0:T(8,128)} copy(f32[2048,256]{1,0:T(8,128)S(1)} %copy-done) | data formatting | bytes 4194304
  52.7 0.0 copy-done.2
  52.7 0.6 %copy.22 = f32[16,256]{1,0:T(8,128)} copy(f32[16,256]{1,0:T(8,128)S(1)} %copy-done.2) | data formatting | bytes 32768
Async XLA Ops:
  2.8 4.9 %copy-start.1 = (f32[2048]{0:T(1024)}, f32[2048]{0:T(1024)S(1)}, u32[]{:S(2)}) copy-start(f32[2048]{0:T(1024)S(1)} %convert_element_type.3) | copy-start | bytes 24580
  49.0 2.4 %copy-start = (f32[2048,256]{1,0:T(8,128)S(1)}, f32[2048,256]{1,0:T(8,128)}, u32[]{:S(2)}) copy-start(f32[2048,256]{1,0:T(8,128)} %get-tuple-element.7) | copy-start | bytes 6291460
  51.4 1.3 %copy-start.2 = (f32[16,256]{1,0:T(8,128)S(1)}, f32[16,256]{1,0:T(8,128)}, u32[]{:S(2)}) copy-start(f32[16,256]{1,0:T(8,128)} %get-tuple-element.8) | copy-start | bytes 49156

commit v3 on v2

--- a/solution.py
+++ b/solution.py
@@ -20,10 +20,10 @@
 
 def whole_kernel(
     peers,
-    index_ref, lists_ref, degree_column_ref, degree_row_ref, features_ref, cotangent_ref,
+    index_ref, lists_ref, hubs_ref, counts_ref, features_ref, cotangent_ref,
     self_ref, neighbour_ref,
     activations_ref, out_ref, weight_out_ref,
-    packed, table, count, summed, edge, part, mean_all, pre_grad, send, returned,
+    packed, table, count, summed, edge, pre_grad_t, mean_all, send, returned, list_row,
     weight_acc, weight_send, weight_in,
     send_sem, recv_sem, back_send_sem, back_recv_sem, weight_send_sem, weight_recv_sem,
 ):
@@ -47,8 +47,37 @@
             barrier, inc=1, device_id=(lax.rem(me + p, peers),), device_id_type=MESH
         )
 
+    per_peer = lists_ref.shape[0]
+    hubs = both - per_peer
+    spread_hubs = jnp.broadcast_to(hubs_ref[...], (8, hubs))
     for start in range(0, remote, 512):
-        rows = lists_ref[start : start + 512, :]
+        row_ids = lax.broadcasted_iota(jnp.int32, (512, peers), 0) + start
+        owner = jnp.where(
+            row_ids // both == lax.broadcasted_iota(jnp.int32, (512, peers), 1), 1.0, 0.0
+        ).astype(BF16)
+        slot = lax.broadcasted_iota(jnp.int32, (512, per_peer), 0) % both
+        own_slot = slot == lax.broadcasted_iota(jnp.int32, (512, per_peer), 1)
+        slot_row = lax.broadcasted_iota(jnp.int32, (per_peer, 512), 1) % both
+        own_slot_row = slot_row == lax.broadcasted_iota(jnp.int32, (per_peer, 512), 0)
+        hub_slot = lax.broadcasted_iota(jnp.int32, (512, hubs), 0) % both - per_peer
+        own_hub = jnp.where(
+            hub_slot == lax.broadcasted_iota(jnp.int32, (512, hubs), 1), 1.0, 0.0
+        ).astype(BF16)
+        column = jnp.zeros((512, 1), F32)
+        line = jnp.zeros((1, 512), F32)
+        for digit, scale in ((lambda v: v >> 8, 256.0), (lambda v: v & 255, 1.0)):
+            sent = digit(lists_ref[...]).astype(F32).astype(BF16)
+            hub = digit(spread_hubs).astype(F32).astype(BF16)
+            by_row = jnp.where(own_slot, dot(owner, sent, 1, 1), 0.0)
+            column = column + scale * (
+                jnp.sum(by_row, axis=1, keepdims=True) + dot(own_hub, hub, 1, 1)[:, :1]
+            )
+            by_column = jnp.where(own_slot_row, dot(sent, owner, 1, 1), 0.0)
+            line = line + scale * (
+                jnp.sum(by_column, axis=0, keepdims=True) + dot(hub, own_hub, 1, 1)[:1]
+            )
+        list_row[:, start : start + 512] = jnp.broadcast_to(line, (8, 512)).astype(jnp.int32)
+        rows = column.astype(jnp.int32)
         ids = lax.broadcasted_iota(jnp.int32, (512, nodes), 1)
         picks = jnp.where(rows == ids, 1.0, 0.0).astype(BF16)
         packed[start : start + 512, :] = dot(picks, features_ref[...], 1, 0).astype(BF16)
@@ -78,11 +107,12 @@
     def _(step):
         groups = BLOCK // 16
         index = index_ref[pl.ds(pl.multiple_of(step * groups, groups), groups), :]
+        highs = (index >> 8).astype(F32)
+        lows = (index & (LO - 1)).astype(F32)
         for group in range(groups):
-            row = index[group : group + 1, :]
-            high = jnp.where(mine, jnp.broadcast_to(row >> 8, (16, lanes)), -1)
-            high = high.astype(F32).astype(BF16)
-            low = jnp.broadcast_to((row & (LO - 1)).astype(F32), (16, lanes)).astype(BF16)
+            high = jnp.broadcast_to(highs[group : group + 1, :], (16, lanes)).astype(BF16)
+            high = jnp.where(mine, high, -one)
+            low = jnp.broadcast_to(lows[group : group + 1, :], (16, lanes)).astype(BF16)
             low = jnp.concatenate([low] * (LO // 16), axis=0)
             low_hot = jnp.where(low_ids == low, one, zero)
             high_hot = jnp.concatenate(
@@ -93,6 +123,9 @@
             at = pl.ds(pl.multiple_of(step * BLOCK + 16 * group, 16), 16)
             for h in range(blocks):
                 count[h, at, :] = counted[16 * h : 16 * h + 16]
+
+    @pl.loop(0, nodes // BLOCK)
+    def _(step):
         at = pl.ds(pl.multiple_of(step * BLOCK, BLOCK), BLOCK)
         total = jnp.zeros((BLOCK, width), F32)
         for h in range(local_blocks):
@@ -110,7 +143,9 @@
             total = total + dot(
                 count[local_blocks + h, at, :], table[h * LO : (h + 1) * LO, :], 1, 0
             )
-        mean = (total / degree_column_ref[at, :]).astype(BF16)
+        degree = counts_ref[:, at].astype(F32)
+        column = jnp.broadcast_to(degree, (128, BLOCK)).T
+        mean = (total / jnp.concatenate([column] * (width // 128), axis=1)).astype(BF16)
         mean_all[at, :] = mean
         pre = dot(features_ref[at, :], self_ref[...], 1, 0) + dot(mean, neighbour_ref[...], 1, 0)
         sig = jax.nn.sigmoid(pre)
@@ -118,9 +153,9 @@
         grad_pre = (
             cotangent_ref[at, :].astype(F32) * sig * (1.0 + pre * (1.0 - sig))
         ).astype(BF16)
-        pre_grad[at, :] = grad_pre
-        edge[:, at] = (dot(neighbour_ref[...], grad_pre, 1, 1) / degree_row_ref[:, at]).astype(BF16)
-        part[:, at] = dot(self_ref[...], grad_pre, 1, 1)
+        pre_grad_t[:, at] = grad_pre.T
+        edge[:, at] = (dot(neighbour_ref[...], grad_pre, 1, 1) / degree).astype(BF16)
+        out_ref[at, :] = dot(grad_pre, self_ref[...], 1, 1)
 
     for h in range(remote_blocks):
         send[h * LO : (h + 1) * LO, :] = dot(edge[...], count[local_blocks + h], 1, 0).T.astype(BF16)
@@ -138,8 +173,8 @@
             device_id_type=MESH,
         ).start()
 
-    weight_acc[:width, :] = dot(features_ref[...], pre_grad[...], 0, 0)
-    weight_acc[width:, :] = dot(mean_all[...], pre_grad[...], 0, 0)
+    weight_acc[:width, :] = dot(pre_grad_t[...], features_ref[...], 1, 0).T
+    weight_acc[width:, :] = dot(pre_grad_t[...], mean_all[...], 1, 0).T
     for p in range(peers):
         weight_send[p] = weight_acc[p * share : (p + 1) * share, :].astype(BF16)
     weight_in[me] = weight_send[me]
@@ -159,16 +194,16 @@
     @pl.loop(0, local_blocks)
     def _(h):
         at = pl.ds(pl.multiple_of(h * LO, LO), LO)
-        part[:, at] = part[:, at] + dot(edge[...], count[h], 1, 0)
+        out_ref[at, :] = out_ref[at, :] + dot(edge[...], count[h], 1, 0).T
 
     pltpu.make_async_copy(returned.at[others], returned.at[others], back_recv_sem).wait()
 
     @pl.loop(0, nodes // BLOCK)
     def _(step):
         at = pl.ds(pl.multiple_of(step * BLOCK, BLOCK), BLOCK)
-        ids = lax.broadcasted_iota(jnp.int32, (remote, BLOCK), 1) + step * BLOCK
-        picks = jnp.where(lists_ref[...] == ids, 1.0, 0.0).astype(BF16)
-        out_ref[at, :] = (part[:, at] + dot(returned[...], picks, 0, 0)).T
+        ids = lax.broadcasted_iota(jnp.int32, (BLOCK, remote), 0) + step * BLOCK
+        picks = jnp.where(list_row[:1, :] == ids, 1.0, 0.0).astype(BF16)
+        out_ref[at, :] = out_ref[at, :] + dot(picks, returned[...], 1, 0)
 
     rest = pl.ds(0, peers - 1)
     pltpu.make_async_copy(weight_in.at[rest], weight_in.at[rest], weight_recv_sem).wait()
@@ -191,9 +226,6 @@
     blocks = (nodes + remote) // LO
     share = 2 * width // peers
 
-    lists = jnp.concatenate(
-        [send_lists[0], jnp.broadcast_to(hub_nodes, (peers, hubs))], axis=1
-    ).reshape(remote, 1)
     past = neighbours - nodes
     hub_past = past - peers * per_peer
     remapped = jnp.where(
@@ -208,7 +240,6 @@
     )
     usable = jnp.arange(fan, dtype=jnp.int32)[None, :] < counts[:, None]
     index = jnp.where(usable, remapped, -1).reshape(nodes // 16, 16 * fan)
-    degree = counts.astype(F32)
     vmem = pl.BlockSpec(memory_space=pltpu.VMEM)
     return pl.pallas_call(
         functools.partial(whole_kernel, peers),
@@ -225,11 +256,11 @@
             pltpu.VMEM((blocks, nodes, LO), BF16),
             pltpu.VMEM((nodes, width), F32),
             pltpu.VMEM((width, nodes), BF16),
-            pltpu.VMEM((width, nodes), F32),
+            pltpu.VMEM((width, nodes), BF16),
             pltpu.VMEM((nodes, width), BF16),
-            pltpu.VMEM((nodes, width), BF16),
-            pltpu.VMEM((remote, width), BF16),
-            pltpu.VMEM((remote, width), BF16),
+            pltpu.VMEM((remote, width), BF16),
+            pltpu.VMEM((remote, width), BF16),
+            pltpu.VMEM((8, remote), jnp.int32),
             pltpu.VMEM((2 * width, width), F32),
             pltpu.VMEM((peers, share, width), BF16),
             pltpu.VMEM((peers, share, width), BF16),
@@ -240,7 +271,7 @@
         ),
         name="whole",
     )(
-        index, lists, degree[:, None], degree[None, :], features, cotangent, self_weight,
+        index, send_lists[0].T, hub_nodes, counts[None, :], features, cotangent, self_weight,
         neighbour_weight,
     )
 

time: 54.2 us -> 46 us (0.85); the launches traced: 53.4 us -> 45.8 us
  Pallas kernels: 41.3 us -> 38.2 us
  local copies, waits for them, and re-layouts: 8.74 us -> 5.73 us
  other arithmetic: 2.64 us -> 1.18 us
    pallas_call x1, Pallas kernels: 41.3 us -> 38.2 us  [body(): pl.pallas_call(functools.partial(whole_kernel, peers), in_specs=[vmem] *...]
    broadcast_in_dim x1 -> x0, local copies, waits for them, and re-layouts: 1.34 us -> none  [body(): degree[:, None]]
    reshape x1 -> x0, local copies, waits for them, and re-layouts: 0.87 us -> none  [body(): lists = jnp.concatenate([send_lists[0], jnp.broadcast_to(hub_nodes, (peer...]
    concatenate x2 -> x0, local copies, waits for them, and re-layouts: 0.8 us -> none  [body(): jnp.concatenate([send_lists[0], jnp.broadcast_to(hub_nodes, (peers, hubs)...]
    concatenate x1 -> x0, other arithmetic: 0.76 us -> none  [body(): jnp.concatenate([send_lists[0], jnp.broadcast_to(hub_nodes, (peers, hubs)...]
    convert_element_type x1 -> x0, other arithmetic: 0.7 us -> none  [body(): degree = counts.astype(F32)]
    unnamed x9 -> x7, local copies, waits for them, and re-layouts: 4.35 us -> 4.34 us
where the time goes in v3:
time: 46 us; the launch traced here: 45.8 us
  Pallas kernels  38.2 us (83%)
  local copies, waits for them, and re-layouts  5.73 us (12%)
  other arithmetic  1.18 us (3%)
  between operations  0.66 us (1%)
    pallas_call x1, Pallas kernels, body(): pl.pallas_call(functools.partial(whole_kernel, peers), in_specs=[vmem] *...  38.2 us
    unnamed x7, local copies, waits for them, and re-layouts  4.34 us
    select_n x1, other arithmetic, body(): index = jnp.where(usable, remapped, -1).reshape(nodes // 16, 16 * fan)  1.18 us
    reshape x1, local copies, waits for them, and re-layouts, body(): index = jnp.where(usable, remapped, -1).reshape(nodes // 16, 16 * fan)  1.06 us

profile of v3, /device:TPU:0, one launch (start us, length us, event | category | flops | bytes accessed | tf_op | source)
XLA Modules:
  0.0 45.8 jit_solution(14347436677633775963)
XLA Ops:
  0.6 1.2 %fusion.5 = s32[2048,16]{0,1:T(8,128)S(1)} fusion(s32[2048,16]{0,1:T(8,128)} %param.13, s32[2048]{0:T(1024)} %param.14), kind=kLoop, calls=%fused_computation.15 | loop fusion | flops 1638400 | bytes 270336 | tf_op jit(solution)/shard_map/jit(_where)/select_n | solution.py:242
  1.8 0.3 copy.12
  2.2 1.1 %reshape.10.index_ref = s32[128,256]{1,0:T(8,128)} reshape(s32[2048,16]{1,0:T(8,128)S(1)} %copy.12) | data formatting | bytes 262144 | tf_op jit(solution)/shard_map/reshape | solution.py:242
  3.2 38.2 %whole.1 = (bf16[2048,256]{1,0:T(8,128)(2,1)}, f32[2048,256]{1,0:T(8,128)}, f32[16,256]{1,0:T(8,128)}) custom-call(s32[128,256]{1,0:T(8,128)} %reshape.10.index_ref, s32[8,32]{1,0:T(8,128)} %bitcast.5, s32[1,8]{1,0:T(1,128)} %hubs_ref.1, s32[1,2048]{1,0:T(1,128)} %bitcast.4, bf16[2048,256]{1,0:T(8,128)(2,1)} %features_ref.1, ...), custom_call_target="tpu_custom_call" | custom-call | tf_op jit(solution)/shard_map/whole/pallas_call | solution.py:244
  41.5 0.0 copy-start
  41.5 2.4 %copy.16 = bf16[2048,256]{1,0:T(8,128)(2,1)} copy(bf16[2048,256]{1,0:T(8,128)(2,1)} %get-tuple-element.6) | data formatting | bytes 2097152
  43.9 0.0 copy-done
  43.9 0.0 copy-start.1
  43.9 1.3 %copy.17 = f32[2048,256]{1,0:T(8,128)} copy(f32[2048,256]{1,0:T(8,128)S(1)} %copy-done) | data formatting | bytes 4194304
  45.2 0.0 copy-done.1
  45.2 0.6 %copy.18 = f32[16,256]{1,0:T(8,128)} copy(f32[16,256]{1,0:T(8,128)S(1)} %copy-done.1) | data formatting | bytes 32768
Async XLA Ops:
  41.5 2.4 %copy-start = (f32[2048,256]{1,0:T(8,128)S(1)}, f32[2048,256]{1,0:T(8,128)}, u32[]{:S(2)}) copy-start(f32[2048,256]{1,0:T(8,128)} %get-tuple-element.7) | copy-start | bytes 6291460
  43.9 1.3 %copy-start.1 = (f32[16,256]{1,0:T(8,128)S(1)}, f32[16,256]{1,0:T(8,128)}, u32[]{:S(2)}) copy-start(f32[16,256]{1,0:T(8,128)} %get-tuple-element.8) | copy-start | bytes 49156

commit v4 on v3

--- a/solution.py
+++ b/solution.py
@@ -18,14 +18,20 @@
     return lax.dot_general(a, b, (((ca,), (cb,)), ((), ())), preferred_element_type=F32)
 
 
+def quotient(value, size):
+    if size & (size - 1) == 0:
+        return value >> (size.bit_length() - 1)
+    return value // size
+
+
 def whole_kernel(
     peers,
     index_ref, lists_ref, hubs_ref, counts_ref, features_ref, cotangent_ref,
     self_ref, neighbour_ref,
-    activations_ref, out_ref, weight_out_ref,
-    packed, table, count, summed, edge, pre_grad_t, mean_all, send, returned, list_row,
+    activations_out, part_out, returned_out, weight_in_out, list_row_out,
+    activations_ref, out_ref, packed, table, count, summed, edge, pre_grad_t, mean_all, send, returned, list_row,
     weight_acc, weight_send, weight_in,
-    send_sem, recv_sem, back_send_sem, back_recv_sem, weight_send_sem, weight_recv_sem,
+    send_sem, recv_sem, back_send_sem, back_recv_sem, weight_send_sem, weight_recv_sem, out_sem,
 ):
     me = lax.axis_index("dom")
     nodes, width = features_ref.shape
@@ -34,8 +40,8 @@
     blocks = count.shape[0]
     local_blocks = nodes // LO
     remote_blocks = blocks - local_blocks
-    lanes = index_ref.shape[1]
-    fan = lanes // 16
+    fan = index_ref.shape[0]
+    lanes = 16 * fan
     share = weight_send.shape[1]
     own = pl.ds(pl.multiple_of(me * both, both), both)
 
@@ -100,19 +106,45 @@
     cols16 = lax.broadcasted_iota(jnp.int32, (16, lanes), 1) // fan
     mine = rows16 == cols16
     low_ids = lax.broadcasted_iota(jnp.int32, (LO, lanes), 0).astype(F32).astype(BF16)
+    mine_block = (
+        lax.broadcasted_iota(jnp.int32, (BLOCK, lanes), 0) & 15
+    ) == lax.broadcasted_iota(jnp.int32, (BLOCK, lanes), 1) // fan
+    to_lanes = jnp.where(
+        lax.broadcasted_iota(jnp.int32, (fan, lanes), 0)
+        == lax.broadcasted_iota(jnp.int32, (fan, lanes), 1) % fan,
+        1.0,
+        0.0,
+    ).astype(BF16)
+    same_group = jnp.where(
+        lax.broadcasted_iota(jnp.int32, (BLOCK, BLOCK), 0) >> 4
+        == lax.broadcasted_iota(jnp.int32, (BLOCK, BLOCK), 1) >> 4,
+        1.0,
+        0.0,
+    ).astype(BF16)
     one = jnp.ones((), BF16)
     zero = jnp.zeros((), BF16)
 
     @pl.loop(0, nodes // BLOCK)
     def _(step):
         groups = BLOCK // 16
-        index = index_ref[pl.ds(pl.multiple_of(step * groups, groups), groups), :]
-        highs = (index >> 8).astype(F32)
-        lows = (index & (LO - 1)).astype(F32)
+        here = pl.ds(pl.multiple_of(step * BLOCK, BLOCK), BLOCK)
+        slots = index_ref[:, here]
+        past = slots - nodes
+        hub_past = past - peers * per_peer
+        sent_at = quotient(past, per_peer)
+        sent_at = sent_at * both + (past - sent_at * per_peer)
+        hub_at = quotient(hub_past, hubs)
+        hub_at = hub_at * both + per_peer + (hub_past - hub_at * hubs)
+        index = jnp.where(past < 0, slots, nodes + jnp.where(hub_past < 0, sent_at, hub_at))
+        used = lax.broadcasted_iota(jnp.int32, (fan, BLOCK), 0) < counts_ref[:, here]
+        index = jnp.where(used, index, -1)
+        highs = dot((index >> 8).astype(F32).astype(BF16), to_lanes, 0, 0).astype(BF16)
+        lows = dot((index & (LO - 1)).astype(F32).astype(BF16), to_lanes, 0, 0)
+        lows = jnp.where(mine_block, lows, 0.0).astype(BF16)
+        lows = dot(same_group, lows, 1, 0).astype(BF16)
         for group in range(groups):
-            high = jnp.broadcast_to(highs[group : group + 1, :], (16, lanes)).astype(BF16)
-            high = jnp.where(mine, high, -one)
-            low = jnp.broadcast_to(lows[group : group + 1, :], (16, lanes)).astype(BF16)
+            high = jnp.where(mine, highs[16 * group : 16 * group + 16], -one)
+            low = lows[16 * group : 16 * group + 16]
             low = jnp.concatenate([low] * (LO // 16), axis=0)
             low_hot = jnp.where(low_ids == low, one, zero)
             high_hot = jnp.concatenate(
@@ -150,6 +182,9 @@
         pre = dot(features_ref[at, :], self_ref[...], 1, 0) + dot(mean, neighbour_ref[...], 1, 0)
         sig = jax.nn.sigmoid(pre)
         activations_ref[at, :] = (pre * sig).astype(BF16)
+        pltpu.make_async_copy(
+            activations_ref.at[at], activations_out.at[at], out_sem.at[0]
+        ).start()
         grad_pre = (
             cotangent_ref[at, :].astype(F32) * sig * (1.0 + pre * (1.0 - sig))
         ).astype(BF16)
@@ -195,22 +230,40 @@
     def _(h):
         at = pl.ds(pl.multiple_of(h * LO, LO), LO)
         out_ref[at, :] = out_ref[at, :] + dot(edge[...], count[h], 1, 0).T
+        pltpu.make_async_copy(out_ref.at[at], part_out.at[at], out_sem.at[1]).start()
 
     pltpu.make_async_copy(returned.at[others], returned.at[others], back_recv_sem).wait()
 
-    @pl.loop(0, nodes // BLOCK)
-    def _(step):
-        at = pl.ds(pl.multiple_of(step * BLOCK, BLOCK), BLOCK)
-        ids = lax.broadcasted_iota(jnp.int32, (BLOCK, remote), 0) + step * BLOCK
-        picks = jnp.where(list_row[:1, :] == ids, 1.0, 0.0).astype(BF16)
-        out_ref[at, :] = out_ref[at, :] + dot(picks, returned[...], 1, 0)
-
+    back = pltpu.make_async_copy(returned, returned_out, out_sem.at[2])
+    back.start()
     rest = pl.ds(0, peers - 1)
     pltpu.make_async_copy(weight_in.at[rest], weight_in.at[rest], weight_recv_sem).wait()
-    weight_out_ref[...] = jnp.sum(weight_in[...].astype(F32), axis=0)
+    weights = pltpu.make_async_copy(weight_in, weight_in_out, out_sem.at[3])
+    weights.start()
+    list_row_out[...] = list_row[...]
     pltpu.make_async_copy(packed.at[others], packed.at[others], send_sem).wait()
     pltpu.make_async_copy(send.at[others], send.at[others], back_send_sem).wait()
     pltpu.make_async_copy(weight_send.at[rest], weight_send.at[rest], weight_send_sem).wait()
+    pltpu.make_async_copy(activations_ref, activations_out, out_sem.at[0]).wait()
+    pltpu.make_async_copy(out_ref, part_out, out_sem.at[1]).wait()
+    back.wait()
+    weights.wait()
+
+
+def final_kernel(
+    part_ref, list_ref, returned_ref, weight_in_ref, activations_in,
+    out_ref, weight_out_ref, activations_ref,
+):
+    step = pl.program_id(0)
+    rows, remote = out_ref.shape[0], list_ref.shape[1]
+    ids = lax.broadcasted_iota(jnp.int32, (rows, remote), 0) + step * rows
+    picks = jnp.where(list_ref[:1, :] == ids, 1.0, 0.0).astype(BF16)
+    out_ref[...] = part_ref[...] + dot(picks, returned_ref[...], 1, 0)
+    activations_ref[...] = activations_in[...]
+
+    @pl.when(step == 0)
+    def _():
+        weight_out_ref[...] = jnp.sum(weight_in_ref[...].astype(F32), axis=0)
 
 
 def body(
@@ -226,31 +279,22 @@
     blocks = (nodes + remote) // LO
     share = 2 * width // peers
 
-    past = neighbours - nodes
-    hub_past = past - peers * per_peer
-    remapped = jnp.where(
-        past < 0,
-        neighbours,
-        nodes
-        + jnp.where(
-            hub_past < 0,
-            (past // per_peer) * both + past % per_peer,
-            (hub_past // hubs) * both + per_peer + hub_past % hubs,
-        ),
-    )
-    usable = jnp.arange(fan, dtype=jnp.int32)[None, :] < counts[:, None]
-    index = jnp.where(usable, remapped, -1).reshape(nodes // 16, 16 * fan)
     vmem = pl.BlockSpec(memory_space=pltpu.VMEM)
-    return pl.pallas_call(
+    anywhere = pl.BlockSpec(memory_space=pl.ANY)
+    activations, part, returned, weight_in, list_row = pl.pallas_call(
         functools.partial(whole_kernel, peers),
         in_specs=[vmem] * 8,
-        out_specs=[vmem] * 3,
+        out_specs=[anywhere] * 4 + [vmem],
         out_shape=[
             jax.ShapeDtypeStruct((nodes, width), BF16),
             jax.ShapeDtypeStruct((nodes, width), F32),
-            jax.ShapeDtypeStruct((share, width), F32),
+            jax.ShapeDtypeStruct((remote, width), BF16),
+            jax.ShapeDtypeStruct((peers, share, width), BF16),
+            jax.ShapeDtypeStruct((8, remote), jnp.int32),
         ],
         scratch_shapes=[
+            pltpu.VMEM((nodes, width), BF16),
+            pltpu.VMEM((nodes, width), F32),
             pltpu.VMEM((remote, width), BF16),
             pltpu.VMEM((remote, width), BF16),
             pltpu.VMEM((blocks, nodes, LO), BF16),
@@ -265,15 +309,37 @@
             pltpu.VMEM((peers, share, width), BF16),
             pltpu.VMEM((peers, share, width), BF16),
         ]
-        + [pltpu.SemaphoreType.DMA] * 6,
+        + [pltpu.SemaphoreType.DMA] * 6
+        + [pltpu.SemaphoreType.DMA((4,))],
         compiler_params=pltpu.CompilerParams(
             collective_id=0, has_side_effects=True, vmem_limit_bytes=60 * 1024 * 1024
         ),
         name="whole",
     )(
-        index, send_lists[0].T, hub_nodes, counts[None, :], features, cotangent, self_weight,
-        neighbour_weight,
+        neighbours.T, send_lists[0].T, hub_nodes, counts[None, :], features, cotangent,
+        self_weight, neighbour_weight,
     )
+    rows = 512
+    block = pl.BlockSpec((rows, width), lambda i: (i, 0))
+    grad_features, grad_weights, activations = pl.pallas_call(
+        final_kernel,
+        grid=(nodes // rows,),
+        in_specs=[
+            block,
+            pl.BlockSpec((8, remote), lambda i: (0, 0)),
+            pl.BlockSpec((remote, width), lambda i: (0, 0)),
+            pl.BlockSpec((peers, share, width), lambda i: (0, 0, 0)),
+            block,
+        ],
+        out_specs=[block, pl.BlockSpec((share, width), lambda i: (0, 0)), block],
+        out_shape=[
+            jax.ShapeDtypeStruct((nodes, width), F32),
+            jax.ShapeDtypeStruct((share, width), F32),
+            jax.ShapeDtypeStruct((nodes, width), BF16),
+        ],
+        name="final",
+    )(part, list_row, returned, weight_in, activations)
+    return (activations, grad_features, grad_weights)
 
 
 def solution(mesh):

time: 46 us -> 46.8 us (1.017)
  Pallas kernels: 38.2 us -> 45.9 us
  local copies, waits for them, and re-layouts: 5.73 us -> 0 us
  other arithmetic: 1.18 us -> 0 us
    pallas_call x0 -> x1, Pallas kernels: none -> 4.92 us  [body(): pl.pallas_call(final_kernel, grid=(nodes // rows,), in_specs=[block, pl.B...]
    unnamed x7 -> x0, local copies, waits for them, and re-layouts: 4.34 us -> none
    pallas_call x1, Pallas kernels: 38.2 us -> 41 us  [body(): pl.pallas_call(functools.partial(whole_kernel, peers), in_specs=[vmem] *...]
    select_n x1 -> x0, other arithmetic: 1.18 us -> none  [body(): index = jnp.where(usable, remapped, -1).reshape(nodes // 16, 16 * fan)]
    reshape x1 -> x0, local copies, waits for them, and re-layouts: 1.06 us -> none  [body(): index = jnp.where(usable, remapped, -1).reshape(nodes // 16, 16 * fan)]
where the time goes in v4:
time: 46.8 us; the launch traced here: 46.5 us
  Pallas kernels  45.9 us (98%)
  between operations  0.64 us (1%)
    pallas_call x1, Pallas kernels, body(): pl.pallas_call(functools.partial(whole_kernel, peers), in_specs=[vmem] *...  41 us
    pallas_call x1, Pallas kernels, body(): pl.pallas_call(final_kernel, grid=(nodes // rows,), in_specs=[block, pl.B...  4.92 us

profile of v4, /device:TPU:0, one launch (start us, length us, event | category | flops | bytes accessed | tf_op | source)
XLA Modules:
  0.0 46.5 jit_solution(9460937945329653722)
XLA Ops:
  0.6 41.0 %whole.1 = (bf16[2048,256]{1,0:T(8,128)(2,1)}, f32[2048,256]{1,0:T(8,128)}, bf16[512,256]{1,0:T(8,128)(2,1)}, bf16[32,16,256]{2,1,0:T(8,128)(2,1)}, s32[8,512]{1,0:T(8,128)}) custom-call(s32[16,2048]{1,0:T(8,128)} %bitcast.5, s32[8,32]{1,0:T(8,128)} %bitcast.7, s32[1,8]{1,0:T(1,128)} %hubs_ref.1, s32[1,2048]{1,0:T(1,128)} %bitcast.6, ...), custom_call_target="tpu_custom_call" | custom-call | tf_op jit(solution)/shard_map/whole/pallas_call | solution.py:284
  41.6 4.9 %final.1 = (f32[2048,256]{1,0:T(8,128)}, f32[16,256]{1,0:T(8,128)}, bf16[2048,256]{1,0:T(8,128)(2,1)}) custom-call(f32[2048,256]{1,0:T(8,128)} %get-tuple-element.11.part_ref, s32[8,512]{1,0:T(8,128)} %get-tuple-element.12.list_ref, bf16[512,256]{1,0:T(8,128)(2,1)} %get-tuple-element.13.returned_ref, bf16[32,16,256]{2,1,0:T(8,128)(2,1)} %get-tuple-element.14.weight_in_ref, ...), custom_call_target="tpu_custom_call" | custom-call | tf_op jit(solution)/shard_map/final/pallas_call | solution.py:324

commit v5 on v3

--- a/solution.py
+++ b/solution.py
@@ -22,10 +22,10 @@
     peers,
     index_ref, lists_ref, hubs_ref, counts_ref, features_ref, cotangent_ref,
     self_ref, neighbour_ref,
-    activations_ref, out_ref, weight_out_ref,
-    packed, table, count, summed, edge, pre_grad_t, mean_all, send, returned, list_row,
+    activations_out, grads_out, weight_out_ref,
+    activations_ref, out_ref, packed, table, count, summed, edge, pre_grad_t, mean_all, send, returned, list_row,
     weight_acc, weight_send, weight_in,
-    send_sem, recv_sem, back_send_sem, back_recv_sem, weight_send_sem, weight_recv_sem,
+    send_sem, recv_sem, back_send_sem, back_recv_sem, weight_send_sem, weight_recv_sem, out_sem,
 ):
     me = lax.axis_index("dom")
     nodes, width = features_ref.shape
@@ -150,6 +150,9 @@
         pre = dot(features_ref[at, :], self_ref[...], 1, 0) + dot(mean, neighbour_ref[...], 1, 0)
         sig = jax.nn.sigmoid(pre)
         activations_ref[at, :] = (pre * sig).astype(BF16)
+        pltpu.make_async_copy(
+            activations_ref.at[at], activations_out.at[at], out_sem.at[0]
+        ).start()
         grad_pre = (
             cotangent_ref[at, :].astype(F32) * sig * (1.0 + pre * (1.0 - sig))
         ).astype(BF16)
@@ -204,6 +207,7 @@
         ids = lax.broadcasted_iota(jnp.int32, (BLOCK, remote), 0) + step * BLOCK
         picks = jnp.where(list_row[:1, :] == ids, 1.0, 0.0).astype(BF16)
         out_ref[at, :] = out_ref[at, :] + dot(picks, returned[...], 1, 0)
+        pltpu.make_async_copy(out_ref.at[at], grads_out.at[at], out_sem.at[1]).start()
 
     rest = pl.ds(0, peers - 1)
     pltpu.make_async_copy(weight_in.at[rest], weight_in.at[rest], weight_recv_sem).wait()
@@ -211,6 +215,8 @@
     pltpu.make_async_copy(packed.at[others], packed.at[others], send_sem).wait()
     pltpu.make_async_copy(send.at[others], send.at[others], back_send_sem).wait()
     pltpu.make_async_copy(weight_send.at[rest], weight_send.at[rest], weight_send_sem).wait()
+    pltpu.make_async_copy(activations_ref, activations_out, out_sem.at[0]).wait()
+    pltpu.make_async_copy(out_ref, grads_out, out_sem.at[1]).wait()
 
 
 def body(
@@ -244,13 +250,15 @@
     return pl.pallas_call(
         functools.partial(whole_kernel, peers),
         in_specs=[vmem] * 8,
-        out_specs=[vmem] * 3,
+        out_specs=[pl.BlockSpec(memory_space=pl.ANY)] * 2 + [vmem],
         out_shape=[
             jax.ShapeDtypeStruct((nodes, width), BF16),
             jax.ShapeDtypeStruct((nodes, width), F32),
             jax.ShapeDtypeStruct((share, width), F32),
         ],
         scratch_shapes=[
+            pltpu.VMEM((nodes, width), BF16),
+            pltpu.VMEM((nodes, width), F32),
             pltpu.VMEM((remote, width), BF16),
             pltpu.VMEM((remote, width), BF16),
             pltpu.VMEM((blocks, nodes, LO), BF16),
@@ -265,7 +273,8 @@
             pltpu.VMEM((peers, share, width), BF16),
             pltpu.VMEM((peers, share, width), BF16),
         ]
-        + [pltpu.SemaphoreType.DMA] * 6,
+        + [pltpu.SemaphoreType.DMA] * 6
+        + [pltpu.SemaphoreType.DMA((2,))],
         compiler_params=pltpu.CompilerParams(
             collective_id=0, has_side_effects=True, vmem_limit_bytes=60 * 1024 * 1024
         ),

time: 46 us -> 45 us (0.978)
  Pallas kernels: 38.2 us -> 37.3 us
    pallas_call x1, Pallas kernels: 38.2 us -> 37.3 us  [body(): pl.pallas_call(functools.partial(whole_kernel, peers), in_specs=[vmem] *...]
where the time goes in v5:
time: 45 us; the launch traced here: 44.8 us
  Pallas kernels  37.3 us (83%)
  local copies, waits for them, and re-layouts  5.73 us (13%)
  other arithmetic  1.18 us (3%)
  between operations  0.66 us (1%)
    pallas_call x1, Pallas kernels, body(): pl.pallas_call(functools.partial(whole_kernel, peers), in_specs=[vmem] *...  37.3 us
    unnamed x7, local copies, waits for them, and re-layouts  4.34 us
    select_n x1, other arithmetic, body(): index = jnp.where(usable, remapped, -1).reshape(nodes // 16, 16 * fan)  1.18 us
    reshape x1, local copies, waits for them, and re-layouts, body(): index = jnp.where(usable, remapped, -1).reshape(nodes // 16, 16 * fan)  1.06 us

profile of v5, /device:TPU:0, one launch (start us, length us, event | category | flops | bytes accessed | tf_op | source)
XLA Modules:
  0.0 44.8 jit_solution(3625234747002083901)
XLA Ops:
  0.6 1.2 %fusion.5 = s32[2048,16]{0,1:T(8,128)S(1)} fusion(s32[2048,16]{0,1:T(8,128)} %param.13, s32[2048]{0:T(1024)} %param.14), kind=kLoop, calls=%fused_computation.15 | loop fusion | flops 1638400 | bytes 270336 | tf_op jit(solution)/shard_map/jit(_where)/select_n | solution.py:248
  1.8 0.3 copy.12
  2.2 1.1 %reshape.10.index_ref = s32[128,256]{1,0:T(8,128)} reshape(s32[2048,16]{1,0:T(8,128)S(1)} %copy.12) | data formatting | bytes 262144 | tf_op jit(solution)/shard_map/reshape | solution.py:248
  3.2 37.3 %whole.1 = (bf16[2048,256]{1,0:T(8,128)(2,1)}, f32[2048,256]{1,0:T(8,128)}, f32[16,256]{1,0:T(8,128)}) custom-call(s32[128,256]{1,0:T(8,128)} %reshape.10.index_ref, s32[8,32]{1,0:T(8,128)} %bitcast.5, s32[1,8]{1,0:T(1,128)} %hubs_ref.1, s32[1,2048]{1,0:T(1,128)} %bitcast.4, bf16[2048,256]{1,0:T(8,128)(2,1)} %features_ref.1, ...), custom_call_target="tpu_custom_call" | custom-call | tf_op jit(solution)/shard_map/whole/pallas_call | solution.py:250
  40.5 0.0 copy-start
  40.5 2.4 %copy.16 = bf16[2048,256]{1,0:T(8,128)(2,1)} copy(bf16[2048,256]{1,0:T(8,128)(2,1)} %get-tuple-element.6) | data formatting | bytes 2097152
  42.9 0.0 copy-done
  42.9 0.0 copy-start.1
  42.9 1.3 %copy.17 = f32[2048,256]{1,0:T(8,128)} copy(f32[2048,256]{1,0:T(8,128)S(1)} %copy-done) | data formatting | bytes 4194304
  44.2 0.0 copy-done.1
  44.2 0.6 %copy.18 = f32[16,256]{1,0:T(8,128)} copy(f32[16,256]{1,0:T(8,128)S(1)} %copy-done.1) | data formatting | bytes 32768
Async XLA Ops:
  40.5 2.4 %copy-start = (f32[2048,256]{1,0:T(8,128)S(1)}, f32[2048,256]{1,0:T(8,128)}, u32[]{:S(2)}) copy-start(f32[2048,256]{1,0:T(8,128)} %get-tuple-element.7) | copy-start | bytes 6291460
  42.9 1.3 %copy-start.1 = (f32[16,256]{1,0:T(8,128)S(1)}, f32[16,256]{1,0:T(8,128)}, u32[]{:S(2)}) copy-start(f32[16,256]{1,0:T(8,128)} %get-tuple-element.8) | copy-start | bytes 49156
